TPU v7x, 256 devices: a whole 4x4x8 slice. The times are simulated.
256 devices in a mesh: rows: 64 (over y, z, core), feat: 4 (over x).
Axes of the slice: x: 4, y: 4, z: 8, core: 2. Of those that a mesh axis runs over, the one named last changes fastest.
Arguments:
- cells: bfloat16 [8192, 80, 128], P('rows', 'feat'), may hold values from -19 to 19
- block_table: int32 [64], replicated, may hold values from 0 to 7, as said below
- row_live: int32 [8192], replicated, may hold values from 0 to 1, as said below
- row_train: int32 [8192], replicated, may hold values from 0 to 1, as said below
- feat_qkv: bfloat16 [128, 384], replicated, may hold values from -0.5 to 0.5
- feat_out: bfloat16 [128, 128], replicated, may hold values from -0.5 to 0.5
- item_qkv: bfloat16 [128, 384], replicated, may hold values from -0.5 to 0.5
- item_out: bfloat16 [128, 128], replicated, may hold values from -0.5 to 0.5
Outputs:
- layer_output: bfloat16 [8192, 80, 128], P(('rows', 'feat'))
Inputs may be any that keep to these rules, and one draw needn't show every extreme that they name: `block_table`: every table number appears in some block. `row_live`: every training row is live. `row_train`: each aligned group of 32 rows holds 1 to 4 training rows; some group holds exactly 4.
All inputs are finite; a program needn't handle non-finite values.
Results may differ from a plain program's by a relative error of at most 0.014.
Values may be sent and summed in bfloat16 or wider, within the bound.
A program may use at most 64 MiB of HBM per device.

v0:
```python
import jax
import jax.numpy as jnp
from jax import lax
from jax.experimental import pallas as pl
from jax.experimental.pallas import tpu as pltpu
from jax.sharding import PartitionSpec as P

HEADS = 4
HEAD_DIM = 32
WIDTH = 128
KEEP = 4
XS, YS, ZS, CS = 4, 4, 8, 2
BLOCKS = YS * ZS * CS
BLOCK = 128
FEATS = 80
SHARD = 20
OWNED = 5
GROUP = 32
OWNERS = XS * YS
PLACES = ZS * CS
KEYS = YS * XS * KEEP
TILE = 256
EPSILON = 1e-05
MASKED = -1e30
SCALE = HEAD_DIM**-0.5 * 1.4426950408889634
MESH = pl.DeviceIdType.MESH
F32 = jnp.float32
BF16 = jnp.bfloat16
VMEM = pl.BlockSpec(memory_space=pltpu.VMEM)
SMEM = pl.BlockSpec(memory_space=pltpu.SMEM)
ANY = pl.BlockSpec(memory_space=pl.ANY)


def iota(shape, dim):
    return lax.broadcasted_iota(jnp.int32, shape, dim)


def row_of(y, z, c):
    return y * (ZS * CS) + z * CS + c


def around(at, step, size):
    return lax.rem(at + step + size, size)


def remote(source, target, send, recv, row, feat):
    return pltpu.make_async_remote_copy(
        src_ref=source,
        dst_ref=target,
        send_sem=send,
        recv_sem=recv,
        device_id=(row, feat),
        device_id_type=MESH,
    )


def position():
    row = lax.axis_index("rows")
    x = lax.axis_index("feat")
    y = lax.div(row, ZS * CS)
    z = lax.rem(lax.div(row, CS), ZS)
    c = lax.rem(row, CS)
    return row, x, y, z, c


def mix_kernel(
    cells, table, live, train, wqkv, wout, q_out, kv_out,
    own, xbuf, part, level, mean_of, inv_of, st_src, sx, sy_src, sy, sz_src, sz, counts, nrm, rows, qkv, att, mix, send,
    key_wide, key_send, key_in,
    own_sem, xs, xr, ss, sr, ys, yr, zs, zr, ks, kr, qs, qr, rs, rr, ls, lr, ps, pr,
):
    row, x, y, z, c = position()
    owner = y * XS + x

    fetch = pltpu.make_async_copy(cells, own, own_sem.at[0])
    fetch.start()
    barrier = pltpu.get_barrier_semaphore()
    greet = []
    for dy in range(YS):
        for dx in range(XS):
            if dx or dy:
                greet.append((row_of(around(y, dy, YS), z, c), around(x, dx, XS)))
        greet.append((row_of(around(y, dy, YS), z, 1 - c), x))
    for dz in range(1, ZS):
        greet.append((row_of(y, around(z, dz, ZS), c), x))
    for peer in greet:
        pl.semaphore_signal(barrier, inc=1, device_id=peer, device_id_type=MESH)
    fetch.wait()

    square = iota((BLOCK, WIDTH), 0) == iota((BLOCK, WIDTH), 1)
    flags = live[pl.ds(row, 1), :].astype(F32)
    weight = jnp.broadcast_to(
        jnp.sum(jnp.where(square, flags, 0.0), axis=1, keepdims=True), (BLOCK, WIDTH)
    )
    entries = jnp.broadcast_to(jnp.sum(flags, axis=1, keepdims=True) * WIDTH, (SHARD, WIDTH))

    def add_first(f, none):
        part[pl.ds(f, 1), :] = jnp.sum(own[f].astype(F32) * weight, axis=0, keepdims=True)
        return none

    lax.fori_loop(0, SHARD, add_first, 0, unroll=4)
    first = jnp.sum(part[...], axis=1, keepdims=True)
    level[...] = jnp.broadcast_to(first, (SHARD, WIDTH)) / entries

    def add_second(f, none):
        off = own[f].astype(F32) - level[pl.ds(f, 1), :]
        part[pl.ds(f, 1), :] = jnp.sum(off * off * weight, axis=0, keepdims=True)
        return none

    lax.fori_loop(0, SHARD, add_second, 0, unroll=4)
    second = jnp.sum(part[...], axis=1, keepdims=True)
    lane = iota((SHARD, WIDTH), 1)
    sub = iota((SHARD, WIDTH), 0)
    spot = lane == sub + GROUP * x

    def to_row(column):
        return jnp.sum(jnp.where(spot, column, 0.0), axis=0, keepdims=True)

    st_src[...] = jnp.concatenate(
        [to_row(first), to_row(second), jnp.zeros((6, WIDTH), F32)], axis=0
    )
    counts[...] = WIDTH * jnp.dot(
        live[...].astype(F32).astype(BF16),
        jnp.ones((BLOCK, WIDTH), BF16),
        preferred_element_type=F32,
    )
    key_wide[...] = jnp.zeros_like(key_wide)
    pl.semaphore_wait(barrier, len(greet))

    stat_x = []
    for d in range(1, XS):
        copy = remote(st_src, sx.at[x], ss.at[d], sr.at[d], row, around(x, d, XS))
        copy.start()
        stat_x.append(copy)
    bulk = []
    for d in (1, 3, 2):
        to = around(x, d, XS)
        copy = remote(
            cells.at[:, pl.ds(pl.multiple_of(to * GROUP, GROUP), GROUP)],
            xbuf.at[pl.ds(x * SHARD, SHARD)],
            xs.at[d],
            xr.at[d],
            row,
            to,
        )
        copy.start()
        bulk.append((d, copy))
    keep = pltpu.make_async_copy(
        own.at[:, pl.ds(pl.multiple_of(x * GROUP, GROUP), GROUP)],
        xbuf.at[pl.ds(x * SHARD, SHARD)],
        own_sem.at[1],
    )
    keep.start()
    sx[x] = st_src[...]
    for d in range(1, XS):
        came = around(x, -d, XS)
        remote(st_src, sx.at[came], ss.at[d], sr.at[d], row, x).wait_recv()
    merged = sx[0] + sx[1] + sx[2] + sx[3]
    sy_src[...] = merged
    here = y * CS + c
    sy[here] = merged
    stat_y = []
    for dy in range(YS):
        for dc in range(CS):
            if dy or dc:
                k = dy * CS + dc
                to = row_of(around(y, dy, YS), z, around(c, dc, CS))
                copy = remote(sy_src, sy.at[here], ys.at[k], yr.at[k], to, x)
                copy.start()
                stat_y.append(copy)
    for dy in range(YS):
        for dc in range(CS):
            if dy or dc:
                k = dy * CS + dc
                came = around(y, -dy, YS) * CS + around(c, dc, CS)
                remote(sy_src, sy.at[came], ys.at[k], yr.at[k], row, x).wait_recv()
    for k in range(2):
        tile = jnp.concatenate([sy[i, k : k + 1, :] for i in range(YS * CS)], axis=0)
        sz_src[k] = tile
        sz[z, k] = tile
    stat_z = []
    for d in range(1, ZS):
        copy = remote(
            sz_src, sz.at[z], zs.at[d], zr.at[d], row_of(y, around(z, d, ZS), c), x
        )
        copy.start()
        stat_z.append(copy)
    spots = [jnp.int32(0)] * KEEP
    seen = jnp.int32(0)
    for r in range(GROUP):
        flag = train[row * BLOCK + x * GROUP + r]
        for j in range(KEEP):
            spots[j] = jnp.where((flag == 1) & (seen == j), r, spots[j])
        seen = seen + flag
    mine = table[row]
    weights = [jnp.where(table[b] == mine, 1.0, 0.0).astype(F32) for b in range(BLOCKS)]
    entries_all = jnp.zeros((1, WIDTH), F32)
    for b in range(BLOCKS):
        entries_all = entries_all + weights[b] * counts[b : b + 1, :]
    for d in range(1, ZS):
        came = around(z, -d, ZS)
        remote(sz_src, sz.at[came], zs.at[d], zr.at[d], row, x).wait_recv()

    places = [
        (zz, i, row_of(i // CS, zz, i % CS)) for zz in range(ZS) for i in range(YS * CS)
    ]
    acc = jnp.zeros((1, WIDTH), F32)
    for zz, i, b in places:
        acc = acc + weights[b] * sz[zz, 0, i : i + 1, :]
    mean_row = acc / entries_all
    spread = jnp.zeros((1, WIDTH), F32)
    for zz, i, b in places:
        entries_b = counts[b : b + 1, :]
        off = sz[zz, 0, i : i + 1, :] / entries_b - mean_row
        spread = spread + weights[b] * (sz[zz, 1, i : i + 1, :] + entries_b * (off * off))
    inv_row = lax.rsqrt(spread / entries_all + EPSILON)

    for d, _ in bulk:
        came = xbuf.at[pl.ds(around(x, -d, XS) * SHARD, SHARD)]
        remote(came, came, xs.at[d], xr.at[d], row, x).wait_recv()
    keep.wait()
    for s in range(XS):
        pick = lane == sub + GROUP * s
        for ref, values in ((mean_of, mean_row), (inv_of, inv_row)):
            column = jnp.sum(jnp.where(pick, values, 0.0), axis=1, keepdims=True)
            ref[SHARD * s : SHARD * (s + 1), :] = jnp.broadcast_to(column, (SHARD, WIDTH))

    def norm(f, none):
        value = (xbuf[f].astype(F32) - mean_of[pl.ds(f, 1), :]) * inv_of[pl.ds(f, 1), :]
        nrm[pl.ds(pl.multiple_of(f * GROUP, GROUP), GROUP), :] = value.astype(BF16).astype(F32)
        return none

    lax.fori_loop(0, FEATS, norm, 0, unroll=4)

    def by_row(r, none):
        rows[r] = nrm[pl.ds(r, FEATS, stride=GROUP), :].astype(BF16)
        return none

    lax.fori_loop(0, GROUP, by_row, 0, unroll=4)

    def project(i, none):
        some = rows[pl.ds(i * 4, 4)].reshape(4 * FEATS, WIDTH)
        out = jnp.dot(some, wqkv[...], preferred_element_type=F32)
        qkv[pl.ds(i * 4, 4), :, 0:WIDTH] = (
            (out[:, :WIDTH] * SCALE).astype(BF16).reshape(4, FEATS, WIDTH)
        )
        qkv[pl.ds(i * 4, 4), :, WIDTH:] = (
            out[:, WIDTH:].astype(BF16).reshape(4, FEATS, 2 * WIDTH)
        )
        return none

    lax.fori_loop(0, GROUP // 4, project, 0)

    head = iota((FEATS, WIDTH), 1) // HEAD_DIM
    def attended(r):
        query = qkv[r, :, 0:WIDTH]
        key = qkv[r, :, WIDTH : 2 * WIDTH]
        value = qkv[r, :, 2 * WIDTH :]
        keys = jnp.concatenate(
            [jnp.where(head == h, key, jnp.zeros_like(key)) for h in range(HEADS)], axis=0
        )
        values = jnp.concatenate(
            [jnp.where(head == h, value, jnp.zeros_like(value)) for h in range(HEADS)], axis=0
        )
        scores = lax.dot_general(
            keys, query, (((1,), (1,)), ((), ())), preferred_element_type=F32
        )
        shares = []
        for h in range(HEADS):
            some = scores[h * FEATS : (h + 1) * FEATS]
            some = jnp.exp2(some - jnp.max(some, axis=0, keepdims=True))
            shares.append((some * (1.0 / jnp.sum(some, axis=0, keepdims=True))).astype(BF16))
        return lax.dot_general(
            jnp.concatenate(shares, axis=0),
            values,
            (((0,), (0,)), ((), ())),
            preferred_element_type=F32,
        ).astype(BF16)

    found = [attended(spot) for spot in spots]
    for j in range(KEEP):
        out = jnp.dot(found[j], wout[...], preferred_element_type=F32)
        out = out + rows[spots[j]].astype(F32)
        key_wide[pl.ds(KEEP * lax.rem(x, 2) + j, FEATS, stride=8), :] = out
    key_send[...] = key_wide[...].reshape(FEATS, 8, WIDTH).astype(BF16)
    peers = []
    for dy in range(YS):
        for dx in range(XS):
            if dx or dy:
                ty, tx = around(y, dy, YS), around(x, dx, XS)
                peers.append((dy * XS + dx, ty * XS + tx, row_of(ty, z, c), tx))
    sent = []
    key_moved = []
    for k, to, to_row, tx in peers:
        copy = remote(
            key_send.at[pl.ds(to * OWNED, OWNED)], key_in.at[owner], ks.at[k], kr.at[k], to_row, tx
        )
        copy.start()
        key_moved.append(copy)
    key_in[owner] = key_send[pl.ds(owner * OWNED, OWNED)]

    moved = []

    def half(part):
        first_row = part * (GROUP // 2)

        def attend(r, none):
            att[r] = attended(r)
            return none

        lax.fori_loop(first_row, first_row + GROUP // 2, attend, 0, unroll=16)

        def update(i, none):
            some = att[pl.ds(i * 4, 4)].reshape(4 * FEATS, WIDTH)
            out = jnp.dot(some, wout[...], preferred_element_type=F32)
            out = out + rows[pl.ds(i * 4, 4)].reshape(4 * FEATS, WIDTH).astype(F32)
            mix[pl.ds(i * 4 * FEATS, 4 * FEATS), :] = out
            return none

        lax.fori_loop(part * 4, part * 4 + 4, update, 0, unroll=2)

        def turn(f, none):
            send[f, first_row : first_row + GROUP // 2, :] = mix[
                pl.ds(first_row * FEATS + f, GROUP // 2, stride=FEATS), :
            ].astype(BF16)
            return none

        lax.fori_loop(0, FEATS, turn, 0, unroll=8)
        these = pl.ds(first_row, GROUP // 2)
        for k, to, to_row, tx in peers:
            copy = remote(
                send.at[pl.ds(to * OWNED, OWNED), these],
                q_out.at[owner, :, these],
                qs.at[part * OWNERS + k],
                qr.at[part * OWNERS + k],
                to_row,
                tx,
            )
            copy.start()
            moved.append(copy)
        q_out[owner, :, first_row : first_row + GROUP // 2, :] = send[
            pl.ds(owner * OWNED, OWNED), first_row : first_row + GROUP // 2, :
        ]

    half(0)

    for copy in key_moved:
        copy.wait_recv()
    spot_here = z * CS + c
    for yy in range(YS):
        for f in range(OWNED):
            low = key_in[yy * XS, f].astype(F32) + key_in[yy * XS + 1, f].astype(F32)
            high = key_in[yy * XS + 2, f].astype(F32) + key_in[yy * XS + 3, f].astype(F32)
            kv_out[spot_here, f, yy * 16 : yy * 16 + 16, :] = jnp.concatenate(
                [low, high], axis=0
            ).astype(BF16)

    right, left = row_of(y, around(z, 1, ZS), c), row_of(y, around(z, -1, ZS), c)
    other = row_of(y, z, 1 - c)

    def slot(d, f):
        return kv_out.at[around(z, d, ZS) * CS + c, f]

    def over(d, f):
        k = (d + 4) * OWNED + f
        copy = remote(slot(d, f), slot(d, f), ps.at[k], pr.at[k], other, x)
        copy.start()
        sent.append(copy)

    def go_right(k, f):
        k_f = k * OWNED + f
        copy = remote(slot(-k, f), slot(-k, f), rs.at[k_f], rr.at[k_f], right, x)
        copy.start()
        sent.append(copy)

    def go_left(k, f):
        k_f = k * OWNED + f
        copy = remote(slot(k, f), slot(k, f), ls.at[k_f], lr.at[k_f], left, x)
        copy.start()
        sent.append(copy)

    for f in range(OWNED):
        go_right(0, f)
        go_left(0, f)
    for f in range(OWNED):
        over(0, f)

    half(1)

    for k in range(4):
        for f in range(OWNED):
            k_f = k * OWNED + f
            came = slot(-1 - k, f)
            remote(came, came, rs.at[k_f], rr.at[k_f], right, x).wait_recv()
            if k < 3:
                go_right(k + 1, f)
            over(-1 - k, f)
            if k < 3:
                came = slot(1 + k, f)
                remote(came, came, ls.at[k_f], lr.at[k_f], left, x).wait_recv()
                if k < 2:
                    go_left(k + 1, f)
                over(1 + k, f)
    for copy in moved:
        copy.wait_recv()
    for d in range(-4, 4):
        for f in range(OWNED):
            came = kv_out.at[around(z, d, ZS) * CS + 1 - c, f]
            k = (d + 4) * OWNED + f
            remote(came, came, ps.at[k], pr.at[k], other, x).wait_recv()

    for copy in stat_x + [copy for _, copy in bulk] + stat_y + stat_z + key_moved + moved + sent:
        copy.wait_send()


def item_kernel(
    q_in, kv_in, table, train, wqkv, wout, out,
    qp, kvp, kvc, bias, stack, tops, totals, accs, every, chosen,
):
    row, x, y, z, c = position()
    kvc[...] = jnp.zeros_like(kvc)

    def project_q(i, none):
        part = q_in[i].reshape(OWNED * GROUP, WIDTH)
        got = jnp.dot(part, wqkv[:, :WIDTH], preferred_element_type=F32)
        qp[i] = (got * SCALE).astype(BF16).reshape(OWNED, GROUP, WIDTH)
        return none

    lax.fori_loop(0, OWNERS, project_q, 0, unroll=4)

    def project_kv(i, none):
        part = kv_in[i].reshape(OWNED * KEYS, WIDTH)
        got = jnp.dot(part, wqkv[:, WIDTH:], preferred_element_type=F32)
        kvp[i] = got.astype(BF16).reshape(OWNED, KEYS, 2 * WIDTH)
        return none

    lax.fori_loop(0, PLACES, project_kv, 0, unroll=4)

    group = (iota((OWNERS, BLOCK), 1) // GROUP == iota((OWNERS, BLOCK), 0) // KEEP)
    spread = train[...].astype(F32)[:, None, :] * group.astype(F32)[None]
    counts = jnp.dot(
        spread.reshape(BLOCKS * OWNERS, BLOCK).astype(BF16),
        jnp.ones((BLOCK, WIDTH), BF16),
        preferred_element_type=F32,
    )
    number = (iota((BLOCKS * OWNERS, WIDTH), 0) % KEEP).astype(F32)
    every[...] = jnp.where(number < counts, 0.0, MASKED)
    head = iota((BLOCK, WIDTH), 1) // HEAD_DIM

    def one_block(yy, none):
        mine = table[row_of(yy, z, c)]

        n = jnp.int32(0)
        for j in range(BLOCKS):
            chosen[n] = j
            n = n + jnp.where(table[j] == mine, 1, 0)

        def gather(i, none):
            j = chosen[i]
            at = pl.multiple_of(i * 16, 16)
            come = pl.multiple_of(lax.div(j, PLACES) * 16, 16)
            for f in range(OWNED):
                kvc[f, pl.ds(at, 16), :] = kvp[lax.rem(j, PLACES), f, pl.ds(come, 16), :]
            bias[pl.ds(at, 16), :] = every[pl.ds(pl.multiple_of(j * 16, 16), 16), :]
            return none

        lax.fori_loop(0, n, gather, 0)
        tiles = lax.div(n + 15, 16)

        def tail(i, none):
            bias[pl.ds(pl.multiple_of(i * 16, 16), 16), :] = jnp.full((16, WIDTH), MASKED, F32)
            return none

        lax.fori_loop(n, tiles * 16, tail, 0)

        for f in range(OWNED):
            query = jnp.concatenate([qp[yy * XS + xx, f] for xx in range(XS)], axis=0)
            stack[f] = jnp.concatenate(
                [jnp.where(head == h, query, jnp.zeros_like(query)) for h in range(HEADS)],
                axis=0,
            )
        def first_tile():
            mask = jnp.concatenate([bias[0:TILE, :]] * HEADS, axis=1)
            for f in range(OWNED):
                scores = lax.dot_general(
                    kvc[f, 0:TILE, 0:WIDTH],
                    stack[f],
                    (((1,), (1,)), ((), ())),
                    preferred_element_type=F32,
                )
                scores = scores + mask
                top = jnp.max(scores, axis=0, keepdims=True)
                shares = jnp.exp2(scores - top)
                tops[f] = top
                totals[f] = jnp.sum(shares, axis=0, keepdims=True)
                got = lax.dot_general(
                    kvc[f, 0:TILE, WIDTH:],
                    shares.astype(BF16),
                    (((0,), (0,)), ((), ())),
                    preferred_element_type=F32,
                )
                for h in range(HEADS):
                    rows = slice(h * HEAD_DIM, (h + 1) * HEAD_DIM)
                    cols = slice(h * BLOCK, (h + 1) * BLOCK)
                    accs[f, rows, :] = got[rows, cols]

        first_tile()
        def one_tile(kt, none):
            at = pl.multiple_of(kt * TILE, TILE)
            mask = bias[pl.ds(at, TILE), :]
            mask = jnp.concatenate([mask] * HEADS, axis=1)
            for f in range(OWNED):
                top = tops[f]
                scores = lax.dot_general(
                    kvc[f, pl.ds(at, TILE), 0:WIDTH],
                    stack[f],
                    (((1,), (1,)), ((), ())),
                    preferred_element_type=F32,
                )
                scores = scores + mask
                new_top = jnp.maximum(top, jnp.max(scores, axis=0, keepdims=True))
                shares = jnp.exp2(scores - new_top)
                fade = jnp.exp2(top - new_top)
                tops[f] = new_top
                totals[f] = totals[f] * fade + jnp.sum(shares, axis=0, keepdims=True)
                got = lax.dot_general(
                    kvc[f, pl.ds(at, TILE), WIDTH:],
                    shares.astype(BF16),
                    (((0,), (0,)), ((), ())),
                    preferred_element_type=F32,
                )
                for h in range(HEADS):
                    rows = slice(h * HEAD_DIM, (h + 1) * HEAD_DIM)
                    cols = slice(h * BLOCK, (h + 1) * BLOCK)
                    accs[f, rows, :] = accs[f, rows, :] * fade[:, cols] + got[rows, cols]
            return none

        lax.fori_loop(1, tiles, one_tile, 0)
        for f in range(OWNED):
            total = totals[f]
            attended = jnp.concatenate(
                [
                    accs[f, h * HEAD_DIM : (h + 1) * HEAD_DIM, :]
                    * (1.0 / total[:, h * BLOCK : (h + 1) * BLOCK])
                    for h in range(HEADS)
                ],
                axis=0,
            ).astype(BF16)
            got = lax.dot_general(
                attended, wout[...], (((0,), (0,)), ((), ())), preferred_element_type=F32
            )
            for xx in range(XS):
                mixed = q_in[yy * XS + xx, f].astype(F32)
                out[yy * XS + xx, f] = (mixed + got[xx * GROUP : (xx + 1) * GROUP]).astype(BF16)
        return none

    lax.fori_loop(0, YS, one_block, 0)


def back_kernel(done, out, send_sems, recv_sems):
    row, x, y, z, c = position()
    owner = y * XS + x
    barrier = pltpu.get_barrier_semaphore()
    for dy in range(YS):
        for dx in range(XS):
            if dx or dy:
                peer = (row_of(around(y, dy, YS), z, c), around(x, dx, XS))
                pl.semaphore_signal(barrier, inc=1, device_id=peer, device_id_type=MESH)
    pl.semaphore_wait(barrier, OWNERS - 1)
    sent = []
    for dy in range(YS):
        for dx in range(XS):
            if dx or dy:
                k = dy * XS + dx
                ty, tx = around(y, dy, YS), around(x, dx, XS)
                copy = remote(
                    done.at[ty * XS + tx],
                    out.at[owner],
                    send_sems.at[k],
                    recv_sems.at[k],
                    row_of(ty, z, c),
                    tx,
                )
                copy.start()
                sent.append(copy)
    out[owner] = done[owner]
    for copy in sent:
        copy.wait_recv()
    for copy in sent:
        copy.wait_send()


def turn_kernel(rows, out, wide):
    def widen(g, none):
        wide[pl.ds(pl.multiple_of(g * OWNED * GROUP, 32), OWNED * GROUP), :] = (
            rows[g].reshape(OWNED * GROUP, WIDTH).astype(F32)
        )
        return none

    lax.fori_loop(0, OWNERS, widen, 0)

    def turn(r, none):
        out[r] = wide[pl.ds(r, FEATS, stride=GROUP), :].astype(BF16)
        return none

    lax.fori_loop(0, GROUP, turn, 0, unroll=4)


def item_call(query, key, block_table, train, item_qkv, item_out):
    moved = jax.ShapeDtypeStruct((OWNERS, OWNED, GROUP, WIDTH), BF16)
    return pl.pallas_call(
        item_kernel,
        name="item",
        out_shape=moved,
        in_specs=[VMEM, VMEM, SMEM, VMEM, VMEM, VMEM],
        out_specs=VMEM,
        scratch_shapes=[
            pltpu.VMEM((OWNERS, OWNED, GROUP, WIDTH), BF16),
            pltpu.VMEM((PLACES, OWNED, KEYS, 2 * WIDTH), BF16),
            pltpu.VMEM((OWNED, PLACES * KEYS, 2 * WIDTH), BF16),
            pltpu.VMEM((PLACES * KEYS, WIDTH), F32),
            pltpu.VMEM((OWNED, HEADS * BLOCK, WIDTH), BF16),
            pltpu.VMEM((OWNED, 1, HEADS * BLOCK), F32),
            pltpu.VMEM((OWNED, 1, HEADS * BLOCK), F32),
            pltpu.VMEM((OWNED, WIDTH, BLOCK), F32),
            pltpu.VMEM((PLACES * KEYS, WIDTH), F32),
            pltpu.SMEM((BLOCKS + 8,), jnp.int32),
        ],
    )(query, key, block_table, train, item_qkv, item_out)


def on_device(cells, block_table, row_live, row_train, feat_qkv, feat_out, item_qkv, item_out):
    train = row_train.reshape(BLOCKS, BLOCK)
    live = row_live.reshape(BLOCKS, BLOCK)
    by_feature = jnp.transpose(cells, (1, 0, 2))
    dma = pltpu.SemaphoreType.DMA
    moved = jax.ShapeDtypeStruct((OWNERS, OWNED, GROUP, WIDTH), BF16)
    query, key = pl.pallas_call(
        mix_kernel,
        name="mix",
        out_shape=(moved, jax.ShapeDtypeStruct((PLACES, OWNED, KEYS, WIDTH), BF16)),
        in_specs=[ANY, SMEM, VMEM, SMEM, VMEM, VMEM],
        out_specs=(VMEM, VMEM),
        scratch_shapes=[
            pltpu.VMEM((SHARD, BLOCK, WIDTH), BF16),
            pltpu.VMEM((FEATS, GROUP, WIDTH), BF16),
            pltpu.VMEM((SHARD, WIDTH), F32),
            pltpu.VMEM((SHARD, WIDTH), F32),
            pltpu.VMEM((FEATS, WIDTH), F32),
            pltpu.VMEM((FEATS, WIDTH), F32),
            pltpu.VMEM((8, WIDTH), F32),
            pltpu.VMEM((XS, 8, WIDTH), F32),
            pltpu.VMEM((8, WIDTH), F32),
            pltpu.VMEM((YS * CS, 8, WIDTH), F32),
            pltpu.VMEM((2, YS * CS, WIDTH), F32),
            pltpu.VMEM((ZS, 2, YS * CS, WIDTH), F32),
            pltpu.VMEM((BLOCKS, WIDTH), F32),
            pltpu.VMEM((GROUP * FEATS, WIDTH), F32),
            pltpu.VMEM((GROUP, FEATS, WIDTH), BF16),
            pltpu.VMEM((GROUP, FEATS, 3 * WIDTH), BF16),
            pltpu.VMEM((GROUP, FEATS, WIDTH), BF16),
            pltpu.VMEM((GROUP * FEATS, WIDTH), F32),
            pltpu.VMEM((FEATS, GROUP, WIDTH), BF16),
            pltpu.VMEM((FEATS * 8, WIDTH), F32),
            pltpu.VMEM((FEATS, 8, WIDTH), BF16),
            pltpu.VMEM((OWNERS, OWNED, 8, WIDTH), BF16),
            dma((2,)),
            dma((XS,)), dma((XS,)), dma((XS,)), dma((XS,)),
            dma((8,)), dma((8,)), dma((8,)), dma((8,)),
            dma((OWNERS,)), dma((OWNERS,)), dma((2 * OWNERS,)), dma((2 * OWNERS,)),
            dma((4 * OWNED,)), dma((4 * OWNED,)), dma((3 * OWNED,)), dma((3 * OWNED,)),
            dma((8 * OWNED,)), dma((8 * OWNED,)),
        ],
        compiler_params=pltpu.CompilerParams(collective_id=0, has_side_effects=True),
    )(by_feature, block_table, live, row_train, feat_qkv, feat_out)
    done = item_call(query, key, block_table, train, item_qkv, item_out)
    rows = pl.pallas_call(
        back_kernel,
        name="back",
        out_shape=moved,
        in_specs=[VMEM],
        out_specs=VMEM,
        scratch_shapes=[dma((OWNERS,)), dma((OWNERS,))],
        compiler_params=pltpu.CompilerParams(collective_id=1, has_side_effects=True),
    )(done)
    return pl.pallas_call(
        turn_kernel,
        name="turn",
        out_shape=jax.ShapeDtypeStruct((GROUP, FEATS, WIDTH), BF16),
        in_specs=[VMEM],
        out_specs=VMEM,
        scratch_shapes=[pltpu.VMEM((FEATS * GROUP, WIDTH), F32)],
    )(rows)


def solution(mesh):
    return jax.shard_map(
        on_device,
        mesh=mesh,
        in_specs=(P("rows", "feat", None), P(), P(), P(), P(), P(), P(), P()),
        out_specs=P(("rows", "feat"), None, None),
        check_vma=False,
    )
```

profile of v0, /device:TPU:1, one launch (start us, length us, event | category | flops | bytes accessed | tf_op | source)
XLA Modules:
  0.0 85.6 jit_solution(18017479658424955171)
XLA Ops:
  0.0 53.6 %mix.1 = (bf16[16,5,32,128]{3,2,1,0:T(8,128)(2,1)}, bf16[16,5,64,128]{3,2,1,0:T(8,128)(2,1)}) custom-call(bf16[20,128,128]{2,1,0:T(8,128)(2,1)} %bitcast.3, s32[64]{0:T(128)} %table.3, s32[64,128]{1,0:T(8,128)} %bitcast.5, s32[8192]{0:T(1024)} %train.1, bf16[128,384]{1,0:T(8,128)(2,1)} %wqkv.2, bf16[128,128]{1,0:T(8,128)(2,1)} %wout.2), custom_call_target="tpu_custom_call" | custom-call | tf_op jit(solution)/shard_map/mix/pallas_call | solution.py:638
  53.6 14.1 %item.1.done = bf16[16,5,32,128]{3,2,1,0:T(8,128)(2,1)} custom-call(bf16[16,5,32,128]{3,2,1,0:T(8,128)(2,1)} %get-tuple-element.7.q_in, bf16[16,5,64,128]{3,2,1,0:T(8,128)(2,1)} %get-tuple-element.8.kv_in, s32[64]{0:T(128)} %table.3, s32[64,128]{1,0:T(8,128)} %bitcast.4, bf16[128,384]{1,0:T(8,128)(2,1)} %wqkv.3, bf16[128,128]{1,0:T(8,128)(2,1)} %wout.3), custom_call_target="tpu_custom_call" | custom-call | tf_op jit(solution)/shard_map/item/pallas_call | solution.py:611
  67.7 14.8 %back.1.rows = bf16[16,5,32,128]{3,2,1,0:T(8,128)(2,1)} custom-call(bf16[16,5,32,128]{3,2,1,0:T(8,128)(2,1)} %item.1.done), custom_call_target="tpu_custom_call" | custom-call | tf_op jit(solution)/shard_map/back/pallas_call | solution.py:677
  82.6 3.0 %turn.1 = bf16[32,80,128]{2,1,0:T(8,128)(2,1)} custom-call(bf16[16,5,32,128]{3,2,1,0:T(8,128)(2,1)} %back.1.rows), custom_call_target="tpu_custom_call" | custom-call | tf_op jit(solution)/shard_map/turn/pallas_call | solution.py:686
where the time goes:
time: 85.9 us; the launch traced here: 85.6 us
  Pallas kernels  85.6 us (100%)
    pallas_call x1, Pallas kernels, on_device(): pl.pallas_call(mix_kernel, name='mix', out_shape=(moved, jax.ShapeDtypeSt...  53.6 us
    pallas_call x1, Pallas kernels, on_device(): pl.pallas_call(back_kernel, name='back', out_shape=moved, in_specs=[VMEM]...  14.8 us
    pallas_call x1, Pallas kernels, item_call(): pl.pallas_call(item_kernel, name='item', out_shape=moved, in_specs=[VMEM,...  14.1 us
    pallas_call x1, Pallas kernels, on_device(): pl.pallas_call(turn_kernel, name='turn', out_shape=jax.ShapeDtypeStruct((...  3.03 us

commit v1 on v0

--- a/solution.py
+++ b/solution.py
@@ -24,6 +24,9 @@
 MASKED = -1e30
 SCALE = HEAD_DIM**-0.5 * 1.4426950408889634
 MESH = pl.DeviceIdType.MESH
+MIX_VMEM = 20 << 20
+ITEM_VMEM = 20 << 20
+BACK_VMEM = 8 << 20
 F32 = jnp.float32
 BF16 = jnp.bfloat16
 VMEM = pl.BlockSpec(memory_space=pltpu.VMEM)
@@ -557,53 +560,53 @@
     lax.fori_loop(0, YS, one_block, 0)
 
 
-def back_kernel(done, out, send_sems, recv_sems):
+def back_kernel(done, out, landed, wide, send_sems, recv_sems, own_sem):
     row, x, y, z, c = position()
     owner = y * XS + x
     barrier = pltpu.get_barrier_semaphore()
-    for dy in range(YS):
-        for dx in range(XS):
-            if dx or dy:
-                peer = (row_of(around(y, dy, YS), z, c), around(x, dx, XS))
-                pl.semaphore_signal(barrier, inc=1, device_id=peer, device_id_type=MESH)
+    steps = [(dy, dx) for dy in range(YS) for dx in range(XS) if dx or dy]
+    steps.sort(key=lambda step: min(step[0], YS - step[0]) + min(step[1], XS - step[1]))
+    for dy, dx in steps:
+        peer = (row_of(around(y, dy, YS), z, c), around(x, dx, XS))
+        pl.semaphore_signal(barrier, inc=1, device_id=peer, device_id_type=MESH)
+    keep = pltpu.make_async_copy(done.at[owner], landed.at[owner], own_sem.at[0])
+    keep.start()
     pl.semaphore_wait(barrier, OWNERS - 1)
     sent = []
-    for dy in range(YS):
-        for dx in range(XS):
-            if dx or dy:
-                k = dy * XS + dx
-                ty, tx = around(y, dy, YS), around(x, dx, XS)
-                copy = remote(
-                    done.at[ty * XS + tx],
-                    out.at[owner],
-                    send_sems.at[k],
-                    recv_sems.at[k],
-                    row_of(ty, z, c),
-                    tx,
-                )
-                copy.start()
-                sent.append(copy)
-    out[owner] = done[owner]
-    for copy in sent:
-        copy.wait_recv()
+    for dy, dx in steps:
+        k = dy * XS + dx
+        ty, tx = around(y, dy, YS), around(x, dx, XS)
+        copy = remote(
+            done.at[ty * XS + tx],
+            landed.at[owner],
+            send_sems.at[k],
+            recv_sems.at[k],
+            row_of(ty, z, c),
+            tx,
+        )
+        copy.start()
+        sent.append(copy)
+
+    def place(g):
+        for f in range(OWNED):
+            wide[pl.ds(g * OWNED + f, GROUP, stride=FEATS), :] = landed[g, f].astype(F32)
+
+    keep.wait()
+    place(owner)
+    for dy, dx in steps:
+        k = dy * XS + dx
+        g = around(y, -dy, YS) * XS + around(x, -dx, XS)
+        remote(landed.at[g], landed.at[g], send_sems.at[k], recv_sems.at[k], row, x).wait_recv()
+        place(g)
+
+    def finish(i, none):
+        some = wide[pl.ds(pl.multiple_of(i * 4 * FEATS, 64), 4 * FEATS), :]
+        out[pl.ds(i * 4, 4)] = some.reshape(4, FEATS, WIDTH).astype(BF16)
+        return none
+
+    lax.fori_loop(0, GROUP // 4, finish, 0, unroll=2)
     for copy in sent:
         copy.wait_send()
-
-
-def turn_kernel(rows, out, wide):
-    def widen(g, none):
-        wide[pl.ds(pl.multiple_of(g * OWNED * GROUP, 32), OWNED * GROUP), :] = (
-            rows[g].reshape(OWNED * GROUP, WIDTH).astype(F32)
-        )
-        return none
-
-    lax.fori_loop(0, OWNERS, widen, 0)
-
-    def turn(r, none):
-        out[r] = wide[pl.ds(r, FEATS, stride=GROUP), :].astype(BF16)
-        return none
-
-    lax.fori_loop(0, GROUP, turn, 0, unroll=4)
 
 
 def item_call(query, key, block_table, train, item_qkv, item_out):
@@ -626,6 +629,7 @@
             pltpu.VMEM((PLACES * KEYS, WIDTH), F32),
             pltpu.SMEM((BLOCKS + 8,), jnp.int32),
         ],
+        compiler_params=pltpu.CompilerParams(vmem_limit_bytes=ITEM_VMEM),
     )(query, key, block_table, train, item_qkv, item_out)
 
 
@@ -671,26 +675,26 @@
             dma((4 * OWNED,)), dma((4 * OWNED,)), dma((3 * OWNED,)), dma((3 * OWNED,)),
             dma((8 * OWNED,)), dma((8 * OWNED,)),
         ],
-        compiler_params=pltpu.CompilerParams(collective_id=0, has_side_effects=True),
+        compiler_params=pltpu.CompilerParams(
+            collective_id=0, has_side_effects=True, vmem_limit_bytes=MIX_VMEM
+        ),
     )(by_feature, block_table, live, row_train, feat_qkv, feat_out)
     done = item_call(query, key, block_table, train, item_qkv, item_out)
-    rows = pl.pallas_call(
+    return pl.pallas_call(
         back_kernel,
         name="back",
-        out_shape=moved,
-        in_specs=[VMEM],
+        out_shape=jax.ShapeDtypeStruct((GROUP, FEATS, WIDTH), BF16),
+        in_specs=[ANY],
         out_specs=VMEM,
-        scratch_shapes=[dma((OWNERS,)), dma((OWNERS,))],
-        compiler_params=pltpu.CompilerParams(collective_id=1, has_side_effects=True),
+        scratch_shapes=[
+            pltpu.VMEM((OWNERS, OWNED, GROUP, WIDTH), BF16),
+            pltpu.VMEM((GROUP * FEATS, WIDTH), F32),
+            dma((OWNERS,)), dma((OWNERS,)), dma((1,)),
+        ],
+        compiler_params=pltpu.CompilerParams(
+            collective_id=1, has_side_effects=True, vmem_limit_bytes=BACK_VMEM
+        ),
     )(done)
-    return pl.pallas_call(
-        turn_kernel,
-        name="turn",
-        out_shape=jax.ShapeDtypeStruct((GROUP, FEATS, WIDTH), BF16),
-        in_specs=[VMEM],
-        out_specs=VMEM,
-        scratch_shapes=[pltpu.VMEM((FEATS * GROUP, WIDTH), F32)],
-    )(rows)
 
 
 def solution(mesh):

time: 85.9 us -> 86.1 us (level)
  the two profiles are of different devices: /device:TPU:1 before, /device:TPU:8 now
where the time goes in v1:
time: 86.1 us; the launch traced here: 85.3 us
  Pallas kernels  77.8 us (90%)
  local copies, waits for them, and re-layouts  7.39 us (9%)
    pallas_call x1, Pallas kernels, on_device(): pl.pallas_call(mix_kernel, name='mix', out_shape=(moved, jax.ShapeDtypeSt...  49.9 us
    pallas_call x1, Pallas kernels, item_call(): pl.pallas_call(item_kernel, name='item', out_shape=moved, in_specs=[VMEM,...  16.3 us
    pallas_call x1, Pallas kernels, on_device(): pl.pallas_call(back_kernel, name='back', out_shape=jax.ShapeDtypeStruct((...  11.7 us
    unnamed x17, local copies, waits for them, and re-layouts  7.39 us

profile of v1, /device:TPU:8, one launch (start us, length us, event | category | flops | bytes accessed | tf_op | source)
XLA Modules:
  0.0 85.3 jit_solution(6748342048391401843)
XLA Ops:
  0.0 0.0 copy-start
  0.0 1.1 %copy-done = bf16[128,20,128]{2,0,1:T(8,128)(2,1)S(1)} copy-done((bf16[128,20,128]{2,0,1:T(8,128)(2,1)S(1)}, bf16[128,20,128]{2,0,1:T(8,128)(2,1)}, u32[]{:S(2)}) %copy-start) | copy-done | bytes 655384
  1.1 0.0 copy-start.1
  1.1 0.8 copy-done.1
  1.8 0.0 copy-start.3
  1.8 0.9 %copy-done.3 = bf16[128,384]{1,0:T(8,128)(2,1)S(1)} copy-done((bf16[128,384]{1,0:T(8,128)(2,1)S(1)}, bf16[128,384]{1,0:T(8,128)(2,1)}, u32[]{:S(2)}) %copy-start.3) | copy-done | bytes 98328
  2.7 0.0 copy-start.5
  2.7 0.8 copy-done.5
  3.5 0.0 copy-start.6
  3.5 0.8 copy-done.6
  4.3 0.0 copy-start.7
  4.3 0.7 copy-done.7
  4.9 49.9 %mix.1 = (bf16[16,5,32,128]{3,2,1,0:T(8,128)(2,1)S(1)}, bf16[16,5,64,128]{3,2,1,0:T(8,128)(2,1)S(1)}) custom-call(bf16[20,128,128]{2,1,0:T(8,128)(2,1)S(1)} %bitcast.3, s32[64]{0:T(128)S(1)} %copy-done.7, s32[64,128]{1,0:T(8,128)S(1)} %bitcast.5, s32[8192]{0:T(1024)S(1)} %copy-done.1, bf16[128,384]{1,0:T(8,128)(2,1)S(1)} %copy-done.3, ...), custom_call_target="tpu_custom_call" | custom-call | tf_op jit(solution)/shard_map/mix/pallas_call | solution.py:642
  54.8 0.0 copy-start.2
  54.8 0.9 %copy-done.2 = bf16[128,384]{1,0:T(8,128)(2,1)S(1)} copy-done((bf16[128,384]{1,0:T(8,128)(2,1)S(1)}, bf16[128,384]{1,0:T(8,128)(2,1)}, u32[]{:S(2)}) %copy-start.2) | copy-done | bytes 98328
  55.7 0.0 copy-start.4
  55.7 0.8 copy-done.4
  56.4 16.3 %item.1.done = bf16[16,5,32,128]{3,2,1,0:T(8,128)(2,1)S(1)} custom-call(bf16[16,5,32,128]{3,2,1,0:T(8,128)(2,1)S(1)} %get-tuple-element.7.q_in, bf16[16,5,64,128]{3,2,1,0:T(8,128)(2,1)S(1)} %get-tuple-element.8.kv_in, s32[64]{0:T(128)S(1)} %copy-done.7, s32[64,128]{1,0:T(8,128)S(1)} %bitcast.4, bf16[128,384]{1,0:T(8,128)(2,1)S(1)} %copy-done.2, ...), custom_call_target="tpu_custom_call" | custom-call | tf_op jit(solution)/shard_map/item/pallas_call | solution.py:614
  72.7 11.7 %back.1 = bf16[32,80,128]{2,1,0:T(8,128)(2,1)S(1)} custom-call(bf16[16,5,32,128]{3,2,1,0:T(8,128)(2,1)S(1)} %item.1.done), custom_call_target="tpu_custom_call" | custom-call | tf_op jit(solution)/shard_map/back/pallas_call | solution.py:683
  84.4 0.8 copy.10
Async XLA Ops:
  0.0 1.1 %copy-start = (bf16[128,20,128]{2,0,1:T(8,128)(2,1)S(1)}, bf16[128,20,128]{2,0,1:T(8,128)(2,1)}, u32[]{:S(2)}) copy-start(bf16[128,20,128]{2,0,1:T(8,128)(2,1)} %param.8) | copy-start | bytes 1966084
  1.1 0.8 copy-start.1
  1.8 0.9 %copy-start.3 = (bf16[128,384]{1,0:T(8,128)(2,1)S(1)}, bf16[128,384]{1,0:T(8,128)(2,1)}, u32[]{:S(2)}) copy-start(bf16[128,384]{1,0:T(8,128)(2,1)} %wqkv.2) | copy-start | bytes 294916
  2.7 0.8 copy-start.5
  3.5 0.8 copy-start.6
  4.3 0.7 copy-start.7
  54.8 0.9 %copy-start.2 = (bf16[128,384]{1,0:T(8,128)(2,1)S(1)}, bf16[128,384]{1,0:T(8,128)(2,1)}, u32[]{:S(2)}) copy-start(bf16[128,384]{1,0:T(8,128)(2,1)} %wqkv.3) | copy-start | bytes 294916
  55.7 0.8 copy-start.4

commit v2 on v1

--- a/solution.py
+++ b/solution.py
@@ -32,6 +32,7 @@
 VMEM = pl.BlockSpec(memory_space=pltpu.VMEM)
 SMEM = pl.BlockSpec(memory_space=pltpu.SMEM)
 ANY = pl.BlockSpec(memory_space=pl.ANY)
+HBM = pl.BlockSpec(memory_space=pltpu.HBM)
 
 
 def iota(shape, dim):
@@ -57,6 +58,10 @@
     )
 
 
+def stay(*arrays):
+    return [pltpu.with_memory_space_constraint(a, pltpu.HBM) for a in arrays]
+
+
 def position():
     row = lax.axis_index("rows")
     x = lax.axis_index("feat")
@@ -67,8 +72,8 @@
 
 
 def mix_kernel(
-    cells, table, live, train, wqkv, wout, q_out, kv_out,
-    own, xbuf, part, level, mean_of, inv_of, st_src, sx, sy_src, sy, sz_src, sz, counts, nrm, rows, qkv, att, mix, send,
+    cells, table_in, live_in, train_in, wqkv_in, wout_in, q_out, kv_out,
+    table, live, train, wqkv, wout, in_sem, own, xbuf, part, level, mean_of, inv_of, st_src, sx, sy_src, sy, sz_src, sz, counts, nrm, rows, qkv, att, mix, send,
     key_wide, key_send, key_in,
     own_sem, xs, xr, ss, sr, ys, yr, zs, zr, ks, kr, qs, qr, rs, rr, ls, lr, ps, pr,
 ):
@@ -77,6 +82,14 @@
 
     fetch = pltpu.make_async_copy(cells, own, own_sem.at[0])
     fetch.start()
+    loads = [
+        pltpu.make_async_copy(source, target, in_sem.at[i])
+        for i, (source, target) in enumerate(
+            ((live_in, live), (table_in, table), (train_in, train), (wqkv_in, wqkv), (wout_in, wout))
+        )
+    ]
+    for load in loads:
+        load.start()
     barrier = pltpu.get_barrier_semaphore()
     greet = []
     for dy in range(YS):
@@ -89,6 +102,8 @@
     for peer in greet:
         pl.semaphore_signal(barrier, inc=1, device_id=peer, device_id_type=MESH)
     fetch.wait()
+    for load in loads:
+        load.wait()
 
     square = iota((BLOCK, WIDTH), 0) == iota((BLOCK, WIDTH), 1)
     flags = live[pl.ds(row, 1), :].astype(F32)
@@ -417,11 +432,22 @@
 
 
 def item_kernel(
-    q_in, kv_in, table, train, wqkv, wout, out,
+    q_in, kv_in, table_in, train_in, wqkv_in, wout_in, out,
+    table, train, wqkv, wout, in_sem,
     qp, kvp, kvc, bias, stack, tops, totals, accs, every, chosen,
 ):
     row, x, y, z, c = position()
+    loads = [
+        pltpu.make_async_copy(source, target, in_sem.at[i])
+        for i, (source, target) in enumerate(
+            ((wqkv_in, wqkv), (table_in, table), (train_in, train), (wout_in, wout))
+        )
+    ]
+    for load in loads:
+        load.start()
     kvc[...] = jnp.zeros_like(kvc)
+    for load in loads:
+        load.wait()
 
     def project_q(i, none):
         part = q_in[i].reshape(OWNED * GROUP, WIDTH)
@@ -615,9 +641,14 @@
         item_kernel,
         name="item",
         out_shape=moved,
-        in_specs=[VMEM, VMEM, SMEM, VMEM, VMEM, VMEM],
+        in_specs=[VMEM, VMEM, HBM, HBM, HBM, HBM],
         out_specs=VMEM,
         scratch_shapes=[
+            pltpu.SMEM((BLOCKS,), jnp.int32),
+            pltpu.VMEM((BLOCKS, BLOCK), jnp.int32),
+            pltpu.VMEM((WIDTH, 3 * WIDTH), BF16),
+            pltpu.VMEM((WIDTH, WIDTH), BF16),
+            pltpu.SemaphoreType.DMA((4,)),
             pltpu.VMEM((OWNERS, OWNED, GROUP, WIDTH), BF16),
             pltpu.VMEM((PLACES, OWNED, KEYS, 2 * WIDTH), BF16),
             pltpu.VMEM((OWNED, PLACES * KEYS, 2 * WIDTH), BF16),
@@ -630,7 +661,7 @@
             pltpu.SMEM((BLOCKS + 8,), jnp.int32),
         ],
         compiler_params=pltpu.CompilerParams(vmem_limit_bytes=ITEM_VMEM),
-    )(query, key, block_table, train, item_qkv, item_out)
+    )(query, key, *stay(block_table, train, item_qkv, item_out))
 
 
 def on_device(cells, block_table, row_live, row_train, feat_qkv, feat_out, item_qkv, item_out):
@@ -643,9 +674,15 @@
         mix_kernel,
         name="mix",
         out_shape=(moved, jax.ShapeDtypeStruct((PLACES, OWNED, KEYS, WIDTH), BF16)),
-        in_specs=[ANY, SMEM, VMEM, SMEM, VMEM, VMEM],
+        in_specs=[HBM] * 6,
         out_specs=(VMEM, VMEM),
         scratch_shapes=[
+            pltpu.SMEM((BLOCKS,), jnp.int32),
+            pltpu.VMEM((BLOCKS, BLOCK), jnp.int32),
+            pltpu.SMEM((BLOCKS * BLOCK,), jnp.int32),
+            pltpu.VMEM((WIDTH, 3 * WIDTH), BF16),
+            pltpu.VMEM((WIDTH, WIDTH), BF16),
+            dma((5,)),
             pltpu.VMEM((SHARD, BLOCK, WIDTH), BF16),
             pltpu.VMEM((FEATS, GROUP, WIDTH), BF16),
             pltpu.VMEM((SHARD, WIDTH), F32),
@@ -678,7 +715,7 @@
         compiler_params=pltpu.CompilerParams(
             collective_id=0, has_side_effects=True, vmem_limit_bytes=MIX_VMEM
         ),
-    )(by_feature, block_table, live, row_train, feat_qkv, feat_out)
+    )(*stay(by_feature, block_table, live, row_train, feat_qkv, feat_out))
     done = item_call(query, key, block_table, train, item_qkv, item_out)
     return pl.pallas_call(
         back_kernel,

time: 86.1 us -> 77.9 us (0.905)
  the two profiles are of different devices: /device:TPU:8 before, /device:TPU:1 now
where the time goes in v2:
time: 77.9 us; the launch traced here: 77.8 us
  Pallas kernels  77 us (99%)
  local copies, waits for them, and re-layouts  0.84 us (1%)
    pallas_call x1, Pallas kernels, on_device(): pl.pallas_call(mix_kernel, name='mix', out_shape=(moved, jax.ShapeDtypeSt...  50.9 us
    pallas_call x1, Pallas kernels, on_device(): pl.pallas_call(back_kernel, name='back', out_shape=jax.ShapeDtypeStruct((...  13.6 us
    pallas_call x1, Pallas kernels, item_call(): pl.pallas_call(item_kernel, name='item', out_shape=moved, in_specs=[VMEM,...  12.5 us

profile of v2, /device:TPU:1, one launch (start us, length us, event | category | flops | bytes accessed | tf_op | source)
XLA Modules:
  0.0 77.8 jit_solution(14149175017149257107)
XLA Ops:
  0.0 50.9 %mix.1 = (bf16[16,5,32,128]{3,2,1,0:T(8,128)(2,1)S(1)}, bf16[16,5,64,128]{3,2,1,0:T(8,128)(2,1)S(1)}) custom-call(bf16[20,128,128]{2,1,0:T(8,128)(2,1)} %bitcast.3, s32[64]{0:T(128)} %table_in.3, s32[64,128]{1,0:T(8,128)} %bitcast.5, s32[8192]{0:T(1024)} %train_in.1, bf16[128,384]{1,0:T(8,128)(2,1)} %wqkv_in.2, bf16[128,128]{1,0:T(8,128)(2,1)} %wout_in.2), custom_call_target="tpu_custom_call" | custom-call | tf_op jit(solution)/shard_map/mix/pallas_call | solution.py:673
  50.9 12.5 %item.1.done = bf16[16,5,32,128]{3,2,1,0:T(8,128)(2,1)S(1)} custom-call(bf16[16,5,32,128]{3,2,1,0:T(8,128)(2,1)S(1)} %get-tuple-element.7.q_in, bf16[16,5,64,128]{3,2,1,0:T(8,128)(2,1)S(1)} %get-tuple-element.8.kv_in, s32[64]{0:T(128)} %table_in.3, s32[64,128]{1,0:T(8,128)} %bitcast.4, bf16[128,384]{1,0:T(8,128)(2,1)} %wqkv_in.3, bf16[128,128]{1,0:T(8,128)(2,1)} %wout_in.3), custom_call_target="tpu_custom_call" | custom-call | tf_op jit(solution)/shard_map/item/pallas_call | solution.py:640
  63.4 13.6 %back.1 = bf16[32,80,128]{2,1,0:T(8,128)(2,1)S(1)} custom-call(bf16[16,5,32,128]{3,2,1,0:T(8,128)(2,1)S(1)} %item.1.done), custom_call_target="tpu_custom_call" | custom-call | tf_op jit(solution)/shard_map/back/pallas_call | solution.py:720
  77.0 0.8 %copy.10 = bf16[32,80,128]{2,1,0:T(8,128)(2,1)} copy(bf16[32,80,128]{2,1,0:T(8,128)(2,1)S(1)} %back.1) | data formatting | bytes 1310720

commit v3 on v2

--- a/solution.py
+++ b/solution.py
@@ -26,7 +26,7 @@
 MESH = pl.DeviceIdType.MESH
 MIX_VMEM = 20 << 20
 ITEM_VMEM = 20 << 20
-BACK_VMEM = 8 << 20
+BACK_VMEM = 12 << 20
 F32 = jnp.float32
 BF16 = jnp.bfloat16
 VMEM = pl.BlockSpec(memory_space=pltpu.VMEM)
@@ -431,21 +431,50 @@
         copy.wait_send()
 
 
-def item_kernel(
-    q_in, kv_in, table_in, train_in, wqkv_in, wout_in, out,
-    table, train, wqkv, wout, in_sem,
-    qp, kvp, kvc, bias, stack, tops, totals, accs, every, chosen,
+def attend_tile(key, value, stacked, mask, top, total, acc):
+    scores = lax.dot_general(
+        key, stacked, (((1,), (1,)), ((), ())), preferred_element_type=F32
+    )
+    scores = scores + mask
+    new_top = jnp.maximum(top, jnp.max(scores, axis=0, keepdims=True))
+    shares = jnp.exp2(scores - new_top)
+    fade = jnp.exp2(top - new_top)
+    total = total * fade + jnp.sum(shares, axis=0, keepdims=True)
+    got = lax.dot_general(
+        value, shares.astype(BF16), (((0,), (0,)), ((), ())), preferred_element_type=F32
+    )
+    parts = []
+    for h in range(HEADS):
+        rows = slice(h * HEAD_DIM, (h + 1) * HEAD_DIM)
+        cols = slice(h * BLOCK, (h + 1) * BLOCK)
+        parts.append(acc[rows] * fade[:, cols] + got[rows, cols])
+    return new_top, total, jnp.concatenate(parts, axis=0)
+
+
+def stack_heads(query):
+    head = iota((BLOCK, WIDTH), 1) // HEAD_DIM
+    return jnp.concatenate(
+        [jnp.where(head == h, query, jnp.zeros_like(query)) for h in range(HEADS)], axis=0
+    )
+
+
+def list_kernel(
+    q_in, kv_in, table_in, train_in, wqkv_in,
+    qp, kv_first, bias_first, tops, totals, accs,
+    table, train, wqkv, in_sem, kvp, kv_more, bias_more, every, chosen,
 ):
     row, x, y, z, c = position()
     loads = [
         pltpu.make_async_copy(source, target, in_sem.at[i])
         for i, (source, target) in enumerate(
-            ((wqkv_in, wqkv), (table_in, table), (train_in, train), (wout_in, wout))
+            ((wqkv_in, wqkv), (table_in, table), (train_in, train))
         )
     ]
     for load in loads:
         load.start()
-    kvc[...] = jnp.zeros_like(kvc)
+    tops[...] = jnp.full_like(tops, MASKED)
+    totals[...] = jnp.zeros_like(totals)
+    accs[...] = jnp.zeros_like(accs)
     for load in loads:
         load.wait()
 
@@ -474,102 +503,131 @@
     )
     number = (iota((BLOCKS * OWNERS, WIDTH), 0) % KEEP).astype(F32)
     every[...] = jnp.where(number < counts, 0.0, MASKED)
-    head = iota((BLOCK, WIDTH), 1) // HEAD_DIM
+    nothing = jnp.zeros((16, 2 * WIDTH), BF16)
+    masked = jnp.full((16, WIDTH), MASKED, F32)
 
     def one_block(yy, none):
         mine = table[row_of(yy, z, c)]
-
         n = jnp.int32(0)
         for j in range(BLOCKS):
             chosen[n] = j
             n = n + jnp.where(table[j] == mine, 1, 0)
+        tiles = lax.div(n + 15, 16)
 
         def gather(i, none):
             j = chosen[i]
             at = pl.multiple_of(i * 16, 16)
             come = pl.multiple_of(lax.div(j, PLACES) * 16, 16)
             for f in range(OWNED):
-                kvc[f, pl.ds(at, 16), :] = kvp[lax.rem(j, PLACES), f, pl.ds(come, 16), :]
-            bias[pl.ds(at, 16), :] = every[pl.ds(pl.multiple_of(j * 16, 16), 16), :]
+                kv_first[yy, f, pl.ds(at, 16), :] = kvp[lax.rem(j, PLACES), f, pl.ds(come, 16), :]
+            bias_first[yy, pl.ds(at, 16), :] = every[pl.ds(pl.multiple_of(j * 16, 16), 16), :]
             return none
 
-        lax.fori_loop(0, n, gather, 0)
-        tiles = lax.div(n + 15, 16)
+        lax.fori_loop(0, jnp.minimum(n, 16), gather, 0)
 
         def tail(i, none):
-            bias[pl.ds(pl.multiple_of(i * 16, 16), 16), :] = jnp.full((16, WIDTH), MASKED, F32)
+            at = pl.multiple_of(i * 16, 16)
+            for f in range(OWNED):
+                kv_first[yy, f, pl.ds(at, 16), :] = nothing
+            bias_first[yy, pl.ds(at, 16), :] = masked
             return none
 
-        lax.fori_loop(n, tiles * 16, tail, 0)
-
+        lax.fori_loop(jnp.minimum(n, 16), 16, tail, 0)
+
+        @pl.when(tiles > 1)
+        def _():
+            def gather_more(i, none):
+                j = chosen[i]
+                at = pl.multiple_of((i - 16) * 16, 16)
+                come = pl.multiple_of(lax.div(j, PLACES) * 16, 16)
+                for f in range(OWNED):
+                    kv_more[f, pl.ds(at, 16), :] = kvp[lax.rem(j, PLACES), f, pl.ds(come, 16), :]
+                bias_more[pl.ds(at, 16), :] = every[pl.ds(pl.multiple_of(j * 16, 16), 16), :]
+                return none
+
+            lax.fori_loop(16, n, gather_more, 0)
+
+            def tail_more(i, none):
+                at = pl.multiple_of((i - 16) * 16, 16)
+                for f in range(OWNED):
+                    kv_more[f, pl.ds(at, 16), :] = nothing
+                bias_more[pl.ds(at, 16), :] = masked
+                return none
+
+            lax.fori_loop(n, tiles * 16, tail_more, 0)
+
+            def one_tile(kt, none):
+                at = pl.multiple_of((kt - 1) * TILE, TILE)
+                mask = jnp.concatenate([bias_more[pl.ds(at, TILE), :]] * HEADS, axis=1)
+                for f in range(OWNED):
+                    query = jnp.concatenate([qp[yy * XS + xx, f] for xx in range(XS)], axis=0)
+                    tops[yy, f], totals[yy, f], accs[yy, f] = attend_tile(
+                        kv_more[f, pl.ds(at, TILE), 0:WIDTH],
+                        kv_more[f, pl.ds(at, TILE), WIDTH:],
+                        stack_heads(query),
+                        mask,
+                        tops[yy, f],
+                        totals[yy, f],
+                        accs[yy, f],
+                    )
+                return none
+
+            lax.fori_loop(1, tiles, one_tile, 0)
+
+        return none
+
+    lax.fori_loop(0, YS, one_block, 0)
+
+
+def back_kernel(
+    q_in, qp, kv_first, bias_first, tops, totals, accs, wout_in, out,
+    wout, done, landed, wide, send_sems, recv_sems, own_sem,
+):
+    row, x, y, z, c = position()
+    owner = y * XS + x
+    load = pltpu.make_async_copy(wout_in, wout, own_sem.at[0])
+    load.start()
+    barrier = pltpu.get_barrier_semaphore()
+    for dy in range(YS):
+        for dx in range(XS):
+            if dx or dy:
+                peer = (row_of(around(y, dy, YS), z, c), around(x, dx, XS))
+                pl.semaphore_signal(barrier, inc=1, device_id=peer, device_id_type=MESH)
+    load.wait()
+    sent = []
+
+    def place(g):
+        for f in range(OWNED):
+            wide[pl.ds(g * OWNED + f, GROUP, stride=FEATS), :] = landed[g, f].astype(F32)
+
+    def take(dy):
+        for dx in (1, 3, 2, 0):
+            if dx or dy:
+                k = dy * XS + dx
+                g = around(y, -dy, YS) * XS + around(x, -dx, XS)
+                remote(
+                    landed.at[g], landed.at[g], send_sems.at[k], recv_sems.at[k], row, x
+                ).wait_recv()
+                place(g)
+
+    order = (2, 1, 3, 0)
+    for turn, dy in enumerate(order):
+        yy = around(y, dy, YS)
+        mask = jnp.concatenate([bias_first[yy]] * HEADS, axis=1)
         for f in range(OWNED):
             query = jnp.concatenate([qp[yy * XS + xx, f] for xx in range(XS)], axis=0)
-            stack[f] = jnp.concatenate(
-                [jnp.where(head == h, query, jnp.zeros_like(query)) for h in range(HEADS)],
-                axis=0,
+            _, total, acc = attend_tile(
+                kv_first[yy, f, :, 0:WIDTH],
+                kv_first[yy, f, :, WIDTH:],
+                stack_heads(query),
+                mask,
+                tops[yy, f],
+                totals[yy, f],
+                accs[yy, f],
             )
-        def first_tile():
-            mask = jnp.concatenate([bias[0:TILE, :]] * HEADS, axis=1)
-            for f in range(OWNED):
-                scores = lax.dot_general(
-                    kvc[f, 0:TILE, 0:WIDTH],
-                    stack[f],
-                    (((1,), (1,)), ((), ())),
-                    preferred_element_type=F32,
-                )
-                scores = scores + mask
-                top = jnp.max(scores, axis=0, keepdims=True)
-                shares = jnp.exp2(scores - top)
-                tops[f] = top
-                totals[f] = jnp.sum(shares, axis=0, keepdims=True)
-                got = lax.dot_general(
-                    kvc[f, 0:TILE, WIDTH:],
-                    shares.astype(BF16),
-                    (((0,), (0,)), ((), ())),
-                    preferred_element_type=F32,
-                )
-                for h in range(HEADS):
-                    rows = slice(h * HEAD_DIM, (h + 1) * HEAD_DIM)
-                    cols = slice(h * BLOCK, (h + 1) * BLOCK)
-                    accs[f, rows, :] = got[rows, cols]
-
-        first_tile()
-        def one_tile(kt, none):
-            at = pl.multiple_of(kt * TILE, TILE)
-            mask = bias[pl.ds(at, TILE), :]
-            mask = jnp.concatenate([mask] * HEADS, axis=1)
-            for f in range(OWNED):
-                top = tops[f]
-                scores = lax.dot_general(
-                    kvc[f, pl.ds(at, TILE), 0:WIDTH],
-                    stack[f],
-                    (((1,), (1,)), ((), ())),
-                    preferred_element_type=F32,
-                )
-                scores = scores + mask
-                new_top = jnp.maximum(top, jnp.max(scores, axis=0, keepdims=True))
-                shares = jnp.exp2(scores - new_top)
-                fade = jnp.exp2(top - new_top)
-                tops[f] = new_top
-                totals[f] = totals[f] * fade + jnp.sum(shares, axis=0, keepdims=True)
-                got = lax.dot_general(
-                    kvc[f, pl.ds(at, TILE), WIDTH:],
-                    shares.astype(BF16),
-                    (((0,), (0,)), ((), ())),
-                    preferred_element_type=F32,
-                )
-                for h in range(HEADS):
-                    rows = slice(h * HEAD_DIM, (h + 1) * HEAD_DIM)
-                    cols = slice(h * BLOCK, (h + 1) * BLOCK)
-                    accs[f, rows, :] = accs[f, rows, :] * fade[:, cols] + got[rows, cols]
-            return none
-
-        lax.fori_loop(1, tiles, one_tile, 0)
-        for f in range(OWNED):
-            total = totals[f]
             attended = jnp.concatenate(
                 [
-                    accs[f, h * HEAD_DIM : (h + 1) * HEAD_DIM, :]
+                    acc[h * HEAD_DIM : (h + 1) * HEAD_DIM]
                     * (1.0 / total[:, h * BLOCK : (h + 1) * BLOCK])
                     for h in range(HEADS)
                 ],
@@ -580,50 +638,29 @@
             )
             for xx in range(XS):
                 mixed = q_in[yy * XS + xx, f].astype(F32)
-                out[yy * XS + xx, f] = (mixed + got[xx * GROUP : (xx + 1) * GROUP]).astype(BF16)
-        return none
-
-    lax.fori_loop(0, YS, one_block, 0)
-
-
-def back_kernel(done, out, landed, wide, send_sems, recv_sems, own_sem):
-    row, x, y, z, c = position()
-    owner = y * XS + x
-    barrier = pltpu.get_barrier_semaphore()
-    steps = [(dy, dx) for dy in range(YS) for dx in range(XS) if dx or dy]
-    steps.sort(key=lambda step: min(step[0], YS - step[0]) + min(step[1], XS - step[1]))
-    for dy, dx in steps:
-        peer = (row_of(around(y, dy, YS), z, c), around(x, dx, XS))
-        pl.semaphore_signal(barrier, inc=1, device_id=peer, device_id_type=MESH)
-    keep = pltpu.make_async_copy(done.at[owner], landed.at[owner], own_sem.at[0])
-    keep.start()
-    pl.semaphore_wait(barrier, OWNERS - 1)
-    sent = []
-    for dy, dx in steps:
-        k = dy * XS + dx
-        ty, tx = around(y, dy, YS), around(x, dx, XS)
-        copy = remote(
-            done.at[ty * XS + tx],
-            landed.at[owner],
-            send_sems.at[k],
-            recv_sems.at[k],
-            row_of(ty, z, c),
-            tx,
-        )
-        copy.start()
-        sent.append(copy)
-
-    def place(g):
-        for f in range(OWNED):
-            wide[pl.ds(g * OWNED + f, GROUP, stride=FEATS), :] = landed[g, f].astype(F32)
-
-    keep.wait()
+                done[yy * XS + xx, f] = (mixed + got[xx * GROUP : (xx + 1) * GROUP]).astype(BF16)
+        if turn == 0:
+            pl.semaphore_wait(barrier, OWNERS - 1)
+        for dx in (2, 1, 3, 0):
+            if dx or dy:
+                k = dy * XS + dx
+                tx = around(x, dx, XS)
+                copy = remote(
+                    done.at[yy * XS + tx],
+                    landed.at[owner],
+                    send_sems.at[k],
+                    recv_sems.at[k],
+                    row_of(yy, z, c),
+                    tx,
+                )
+                copy.start()
+                sent.append(copy)
+        if turn >= 2:
+            take(order[turn - 2])
+    landed[owner] = done[owner]
     place(owner)
-    for dy, dx in steps:
-        k = dy * XS + dx
-        g = around(y, -dy, YS) * XS + around(x, -dx, XS)
-        remote(landed.at[g], landed.at[g], send_sems.at[k], recv_sems.at[k], row, x).wait_recv()
-        place(g)
+    take(order[2])
+    take(order[3])
 
     def finish(i, none):
         some = wide[pl.ds(pl.multiple_of(i * 4 * FEATS, 64), 4 * FEATS), :]
@@ -635,33 +672,35 @@
         copy.wait_send()
 
 
-def item_call(query, key, block_table, train, item_qkv, item_out):
-    moved = jax.ShapeDtypeStruct((OWNERS, OWNED, GROUP, WIDTH), BF16)
+def list_call(query, key, block_table, train, item_qkv):
+    shape = jax.ShapeDtypeStruct
+    state = shape((YS, OWNED, 1, HEADS * BLOCK), F32)
     return pl.pallas_call(
-        item_kernel,
-        name="item",
-        out_shape=moved,
-        in_specs=[VMEM, VMEM, HBM, HBM, HBM, HBM],
-        out_specs=VMEM,
+        list_kernel,
+        name="list",
+        out_shape=(
+            shape((OWNERS, OWNED, GROUP, WIDTH), BF16),
+            shape((YS, OWNED, TILE, 2 * WIDTH), BF16),
+            shape((YS, TILE, WIDTH), F32),
+            state,
+            state,
+            shape((YS, OWNED, WIDTH, BLOCK), F32),
+        ),
+        in_specs=[VMEM, VMEM, HBM, HBM, HBM],
+        out_specs=(VMEM,) * 6,
         scratch_shapes=[
             pltpu.SMEM((BLOCKS,), jnp.int32),
             pltpu.VMEM((BLOCKS, BLOCK), jnp.int32),
             pltpu.VMEM((WIDTH, 3 * WIDTH), BF16),
-            pltpu.VMEM((WIDTH, WIDTH), BF16),
-            pltpu.SemaphoreType.DMA((4,)),
-            pltpu.VMEM((OWNERS, OWNED, GROUP, WIDTH), BF16),
+            pltpu.SemaphoreType.DMA((3,)),
             pltpu.VMEM((PLACES, OWNED, KEYS, 2 * WIDTH), BF16),
             pltpu.VMEM((OWNED, PLACES * KEYS, 2 * WIDTH), BF16),
             pltpu.VMEM((PLACES * KEYS, WIDTH), F32),
-            pltpu.VMEM((OWNED, HEADS * BLOCK, WIDTH), BF16),
-            pltpu.VMEM((OWNED, 1, HEADS * BLOCK), F32),
-            pltpu.VMEM((OWNED, 1, HEADS * BLOCK), F32),
-            pltpu.VMEM((OWNED, WIDTH, BLOCK), F32),
             pltpu.VMEM((PLACES * KEYS, WIDTH), F32),
             pltpu.SMEM((BLOCKS + 8,), jnp.int32),
         ],
         compiler_params=pltpu.CompilerParams(vmem_limit_bytes=ITEM_VMEM),
-    )(query, key, *stay(block_table, train, item_qkv, item_out))
+    )(query, key, *stay(block_table, train, item_qkv))
 
 
 def on_device(cells, block_table, row_live, row_train, feat_qkv, feat_out, item_qkv, item_out):
@@ -716,14 +755,16 @@
             collective_id=0, has_side_effects=True, vmem_limit_bytes=MIX_VMEM
         ),
     )(*stay(by_feature, block_table, live, row_train, feat_qkv, feat_out))
-    done = item_call(query, key, block_table, train, item_qkv, item_out)
+    listed = list_call(query, key, block_table, train, item_qkv)
     return pl.pallas_call(
         back_kernel,
         name="back",
         out_shape=jax.ShapeDtypeStruct((GROUP, FEATS, WIDTH), BF16),
-        in_specs=[ANY],
+        in_specs=[VMEM] * 7 + [HBM],
         out_specs=VMEM,
         scratch_shapes=[
+            pltpu.VMEM((WIDTH, WIDTH), BF16),
+            pltpu.VMEM((OWNERS, OWNED, GROUP, WIDTH), BF16),
             pltpu.VMEM((OWNERS, OWNED, GROUP, WIDTH), BF16),
             pltpu.VMEM((GROUP * FEATS, WIDTH), F32),
             dma((OWNERS,)), dma((OWNERS,)), dma((1,)),
@@ -731,7 +772,7 @@
         compiler_params=pltpu.CompilerParams(
             collective_id=1, has_side_effects=True, vmem_limit_bytes=BACK_VMEM
         ),
-    )(done)
+    )(query, *listed, *stay(item_out))
 
 
 def solution(mesh):

time: 77.9 us -> 75.8 us (0.973)
  Pallas kernels: 77 us -> 74.9 us
    pallas_call x1, Pallas kernels: 12.5 us -> 4.65 us  [list_call(): pl.pallas_call(list_kernel, name='list', out_shape=(shape((OWNERS, OWNED,...]
    pallas_call x1, Pallas kernels: 13.6 us -> 19.4 us  [on_device(): pl.pallas_call(back_kernel, name='back', out_shape=jax.ShapeDtypeStruct((...]
where the time goes in v3:
time: 75.8 us
  Pallas kernels  74.9 us (99%)
  local copies, waits for them, and re-layouts  0.84 us (1%)
    pallas_call x1, Pallas kernels, on_device(): pl.pallas_call(mix_kernel, name='mix', out_shape=(moved, jax.ShapeDtypeSt...  50.9 us
    pallas_call x1, Pallas kernels, on_device(): pl.pallas_call(back_kernel, name='back', out_shape=jax.ShapeDtypeStruct((...  19.4 us
    pallas_call x1, Pallas kernels, list_call(): pl.pallas_call(list_kernel, name='list', out_shape=(shape((OWNERS, OWNED,...  4.65 us

profile of v3, /device:TPU:1, one launch (start us, length us, event | category | flops | bytes accessed | tf_op | source)
XLA Modules:
  0.0 75.8 jit_solution(8712319002592120923)
XLA Ops:
  0.0 50.9 %mix.1 = (bf16[16,5,32,128]{3,2,1,0:T(8,128)(2,1)S(1)}, bf16[16,5,64,128]{3,2,1,0:T(8,128)(2,1)S(1)}) custom-call(bf16[20,128,128]{2,1,0:T(8,128)(2,1)} %bitcast.3, s32[64]{0:T(128)} %table_in.3, s32[64,128]{1,0:T(8,128)} %bitcast.5, s32[8192]{0:T(1024)} %train_in.1, bf16[128,384]{1,0:T(8,128)(2,1)} %wqkv_in.2, bf16[128,128]{1,0:T(8,128)(2,1)} %wout_in.2), custom_call_target="tpu_custom_call" | custom-call | tf_op jit(solution)/shard_map/mix/pallas_call | solution.py:712
  50.9 4.6 %list.1 = (bf16[16,5,32,128]{3,2,1,0:T(8,128)(2,1)S(1)}, bf16[4,5,256,256]{3,2,1,0:T(8,128)(2,1)S(1)}, f32[4,256,128]{2,1,0:T(8,128)S(1)}, f32[4,5,1,512]{3,2,1,...) custom-call(bf16[16,5,32,128]{3,2,1,0:T(8,128)(2,1)S(1)} %get-tuple-element.13.q_in, ...), custom_call_target="tpu_custom_call" | custom-call | tf_op jit(solution)/shard_map/list/pallas_call | solution.py:678
  55.6 19.4 %back.1 = bf16[32,80,128]{2,1,0:T(8,128)(2,1)S(1)} custom-call(bf16[16,5,32,128]{3,2,1,0:T(8,128)(2,1)S(1)} %get-tuple-element.13.q_in, bf16[16,5,32,128]{3,2,1,0:T(8,128)(2,1)S(1)} %get-tuple-element.15.qp, bf16[4,5,256,256]{3,2,1,0:T(8,128)(2,1)S(1)} %get-tuple-element.16.kv_first, f32[4,256,128]{2,1,0:T(8,128)S(1)} %get-tuple-element.17.bias_first, ...), custom_call_target="tpu_custom_call" | custom-call | tf_op jit(solution)/shard_map/back/pallas_call | solution.py:759
  75.0 0.8 %copy.10 = bf16[32,80,128]{2,1,0:T(8,128)(2,1)} copy(bf16[32,80,128]{2,1,0:T(8,128)(2,1)S(1)} %back.1) | data formatting | bytes 1310720

commit v4 on v3

--- a/solution.py
+++ b/solution.py
@@ -24,6 +24,8 @@
 MASKED = -1e30
 SCALE = HEAD_DIM**-0.5 * 1.4426950408889634
 MESH = pl.DeviceIdType.MESH
+CHUNKS = ((0, 1), (1, 1), (2, 1), (3, 1), (4, 1))
+FROM_RIGHT = 3
 MIX_VMEM = 20 << 20
 ITEM_VMEM = 20 << 20
 BACK_VMEM = 12 << 20
@@ -73,9 +75,9 @@
 
 def mix_kernel(
     cells, table_in, live_in, train_in, wqkv_in, wout_in, q_out, kv_out,
-    table, live, train, wqkv, wout, in_sem, own, xbuf, part, level, mean_of, inv_of, st_src, sx, sy_src, sy, sz_src, sz, counts, nrm, rows, qkv, att, mix, send,
+    table, live, train, wqkv, wout, in_sem, own, xbuf, part, level, mean_of, inv_of, st_src, sxy, sz_src, sz, counts, nrm, rows, qkv, att, mix, send,
     key_wide, key_send, key_in,
-    own_sem, xs, xr, ss, sr, ys, yr, zs, zr, ks, kr, qs, qr, rs, rr, ls, lr, ps, pr,
+    own_sem, xs, xr, ss, sr, zs, zr, ks, kr, qs, qr, rs, rr, ls, lr, ps, pr,
 ):
     row, x, y, z, c = position()
     owner = y * XS + x
@@ -92,11 +94,11 @@
         load.start()
     barrier = pltpu.get_barrier_semaphore()
     greet = []
-    for dy in range(YS):
-        for dx in range(XS):
-            if dx or dy:
-                greet.append((row_of(around(y, dy, YS), z, c), around(x, dx, XS)))
-        greet.append((row_of(around(y, dy, YS), z, 1 - c), x))
+    plane = [
+        (dx, dy, dc) for dy in range(YS) for dc in range(CS) for dx in range(XS) if dx or dy or dc
+    ]
+    for dx, dy, dc in plane:
+        greet.append((row_of(around(y, dy, YS), z, around(c, dc, CS)), around(x, dx, XS)))
     for dz in range(1, ZS):
         greet.append((row_of(y, around(z, dz, ZS), c), x))
     for peer in greet:
@@ -135,7 +137,7 @@
         return jnp.sum(jnp.where(spot, column, 0.0), axis=0, keepdims=True)
 
     st_src[...] = jnp.concatenate(
-        [to_row(first), to_row(second), jnp.zeros((6, WIDTH), F32)], axis=0
+        [to_row(first), to_row(second)], axis=0
     )
     counts[...] = WIDTH * jnp.dot(
         live[...].astype(F32).astype(BF16),
@@ -145,11 +147,14 @@
     key_wide[...] = jnp.zeros_like(key_wide)
     pl.semaphore_wait(barrier, len(greet))
 
-    stat_x = []
-    for d in range(1, XS):
-        copy = remote(st_src, sx.at[x], ss.at[d], sr.at[d], row, around(x, d, XS))
+    here = y * CS + c
+    stat_xy = []
+    for dx, dy, dc in plane:
+        k = (dy * CS + dc) * XS + dx
+        to = row_of(around(y, dy, YS), z, around(c, dc, CS))
+        copy = remote(st_src, sxy.at[here, x], ss.at[k], sr.at[k], to, around(x, dx, XS))
         copy.start()
-        stat_x.append(copy)
+        stat_xy.append(copy)
     bulk = []
     for d in (1, 3, 2):
         to = around(x, d, XS)
@@ -169,31 +174,16 @@
         own_sem.at[1],
     )
     keep.start()
-    sx[x] = st_src[...]
-    for d in range(1, XS):
-        came = around(x, -d, XS)
-        remote(st_src, sx.at[came], ss.at[d], sr.at[d], row, x).wait_recv()
-    merged = sx[0] + sx[1] + sx[2] + sx[3]
-    sy_src[...] = merged
-    here = y * CS + c
-    sy[here] = merged
-    stat_y = []
-    for dy in range(YS):
-        for dc in range(CS):
-            if dy or dc:
-                k = dy * CS + dc
-                to = row_of(around(y, dy, YS), z, around(c, dc, CS))
-                copy = remote(sy_src, sy.at[here], ys.at[k], yr.at[k], to, x)
-                copy.start()
-                stat_y.append(copy)
-    for dy in range(YS):
-        for dc in range(CS):
-            if dy or dc:
-                k = dy * CS + dc
-                came = around(y, -dy, YS) * CS + around(c, dc, CS)
-                remote(sy_src, sy.at[came], ys.at[k], yr.at[k], row, x).wait_recv()
+    sxy[here, x] = st_src[...]
+    for dx, dy, dc in plane:
+        k = (dy * CS + dc) * XS + dx
+        came = sxy.at[around(y, -dy, YS) * CS + around(c, dc, CS), around(x, -dx, XS)]
+        remote(came, came, ss.at[k], sr.at[k], row, x).wait_recv()
+    merged = [
+        sxy[i, 0] + sxy[i, 1] + sxy[i, 2] + sxy[i, 3] for i in range(YS * CS)
+    ]
     for k in range(2):
-        tile = jnp.concatenate([sy[i, k : k + 1, :] for i in range(YS * CS)], axis=0)
+        tile = jnp.concatenate([merged[i][k : k + 1] for i in range(YS * CS)], axis=0)
         sz_src[k] = tile
         sz[z, k] = tile
     stat_z = []
@@ -248,13 +238,13 @@
         nrm[pl.ds(pl.multiple_of(f * GROUP, GROUP), GROUP), :] = value.astype(BF16).astype(F32)
         return none
 
-    lax.fori_loop(0, FEATS, norm, 0, unroll=4)
+    lax.fori_loop(0, FEATS, norm, 0, unroll=8)
 
     def by_row(r, none):
         rows[r] = nrm[pl.ds(r, FEATS, stride=GROUP), :].astype(BF16)
         return none
 
-    lax.fori_loop(0, GROUP, by_row, 0, unroll=4)
+    lax.fori_loop(0, GROUP, by_row, 0, unroll=8)
 
     def project(i, none):
         some = rows[pl.ds(i * 4, 4)].reshape(4 * FEATS, WIDTH)
@@ -267,7 +257,7 @@
         )
         return none
 
-    lax.fori_loop(0, GROUP // 4, project, 0)
+    lax.fori_loop(0, GROUP // 4, project, 0, unroll=4)
 
     head = iota((FEATS, WIDTH), 1) // HEAD_DIM
     def attended(r):
@@ -376,58 +366,62 @@
     right, left = row_of(y, around(z, 1, ZS), c), row_of(y, around(z, -1, ZS), c)
     other = row_of(y, z, 1 - c)
 
-    def slot(d, f):
-        return kv_out.at[around(z, d, ZS) * CS + c, f]
-
-    def over(d, f):
-        k = (d + 4) * OWNED + f
-        copy = remote(slot(d, f), slot(d, f), ps.at[k], pr.at[k], other, x)
+    count = len(CHUNKS)
+
+    def slot(d, i):
+        return kv_out.at[around(z, d, ZS) * CS + c, pl.ds(CHUNKS[i][0], CHUNKS[i][1])]
+
+    def hop(d, i, sems, k, to):
+        send_sems, recv_sems = sems
+        at = k * count + i
+        copy = remote(slot(d, i), slot(d, i), send_sems.at[at], recv_sems.at[at], to, x)
         copy.start()
         sent.append(copy)
 
-    def go_right(k, f):
-        k_f = k * OWNED + f
-        copy = remote(slot(-k, f), slot(-k, f), rs.at[k_f], rr.at[k_f], right, x)
-        copy.start()
-        sent.append(copy)
-
-    def go_left(k, f):
-        k_f = k * OWNED + f
-        copy = remote(slot(k, f), slot(k, f), ls.at[k_f], lr.at[k_f], left, x)
-        copy.start()
-        sent.append(copy)
-
-    for f in range(OWNED):
-        go_right(0, f)
-        go_left(0, f)
-    for f in range(OWNED):
-        over(0, f)
+    def lands(d, i, sems, k, to):
+        at = k * count + i
+        remote(slot(d, i), slot(d, i), sems[0].at[at], sems[1].at[at], to, x).wait_recv()
+
+    def over(d, i):
+        hop(d, i, (ps, pr), d + 4, other)
+
+    def on_right(k, i):
+        return k < 3 or (k == 3 and i < FROM_RIGHT)
+
+    def on_left(k, i):
+        return k < 3 or (k == 3 and i >= FROM_RIGHT)
+
+    for i in range(count):
+        hop(0, i, (rs, rr), 0, right)
+        hop(0, i, (ls, lr), 0, left)
+    for i in range(count):
+        over(0, i)
 
     half(1)
 
     for k in range(4):
-        for f in range(OWNED):
-            k_f = k * OWNED + f
-            came = slot(-1 - k, f)
-            remote(came, came, rs.at[k_f], rr.at[k_f], right, x).wait_recv()
-            if k < 3:
-                go_right(k + 1, f)
-            over(-1 - k, f)
-            if k < 3:
-                came = slot(1 + k, f)
-                remote(came, came, ls.at[k_f], lr.at[k_f], left, x).wait_recv()
-                if k < 2:
-                    go_left(k + 1, f)
-                over(1 + k, f)
+        for i in range(count):
+            if on_right(k, i):
+                lands(-1 - k, i, (rs, rr), k, right)
+                if on_right(k + 1, i):
+                    hop(-1 - k, i, (rs, rr), k + 1, right)
+                over(-1 - k, i)
+            if on_left(k, i):
+                lands(1 + k, i, (ls, lr), k, left)
+                if on_left(k + 1, i):
+                    hop(1 + k, i, (ls, lr), k + 1, left)
+                over(1 + k if k < 3 else -4, i)
     for copy in moved:
         copy.wait_recv()
     for d in range(-4, 4):
-        for f in range(OWNED):
-            came = kv_out.at[around(z, d, ZS) * CS + 1 - c, f]
-            k = (d + 4) * OWNED + f
-            remote(came, came, ps.at[k], pr.at[k], other, x).wait_recv()
-
-    for copy in stat_x + [copy for _, copy in bulk] + stat_y + stat_z + key_moved + moved + sent:
+        for i in range(count):
+            came = kv_out.at[
+                around(z, d, ZS) * CS + 1 - c, pl.ds(CHUNKS[i][0], CHUNKS[i][1])
+            ]
+            at = (d + 4) * count + i
+            remote(came, came, ps.at[at], pr.at[at], other, x).wait_recv()
+
+    for copy in stat_xy + [copy for _, copy in bulk] + stat_z + key_moved + moved + sent:
         copy.wait_send()
 
 
@@ -728,10 +722,8 @@
             pltpu.VMEM((SHARD, WIDTH), F32),
             pltpu.VMEM((FEATS, WIDTH), F32),
             pltpu.VMEM((FEATS, WIDTH), F32),
-            pltpu.VMEM((8, WIDTH), F32),
-            pltpu.VMEM((XS, 8, WIDTH), F32),
-            pltpu.VMEM((8, WIDTH), F32),
-            pltpu.VMEM((YS * CS, 8, WIDTH), F32),
+            pltpu.VMEM((2, WIDTH), F32),
+            pltpu.VMEM((YS * CS, XS, 2, WIDTH), F32),
             pltpu.VMEM((2, YS * CS, WIDTH), F32),
             pltpu.VMEM((ZS, 2, YS * CS, WIDTH), F32),
             pltpu.VMEM((BLOCKS, WIDTH), F32),
@@ -745,10 +737,10 @@
             pltpu.VMEM((FEATS, 8, WIDTH), BF16),
             pltpu.VMEM((OWNERS, OWNED, 8, WIDTH), BF16),
             dma((2,)),
-            dma((XS,)), dma((XS,)), dma((XS,)), dma((XS,)),
-            dma((8,)), dma((8,)), dma((8,)), dma((8,)),
+            dma((XS,)), dma((XS,)), dma((OWNERS * CS,)), dma((OWNERS * CS,)),
+            dma((8,)), dma((8,)),
             dma((OWNERS,)), dma((OWNERS,)), dma((2 * OWNERS,)), dma((2 * OWNERS,)),
-            dma((4 * OWNED,)), dma((4 * OWNED,)), dma((3 * OWNED,)), dma((3 * OWNED,)),
+            dma((4 * OWNED,)), dma((4 * OWNED,)), dma((4 * OWNED,)), dma((4 * OWNED,)),
             dma((8 * OWNED,)), dma((8 * OWNED,)),
         ],
         compiler_params=pltpu.CompilerParams(

time: 75.8 us -> 72 us (0.950); the launches traced: 75.8 us -> 71.2 us
  Pallas kernels: 74.9 us -> 70.3 us
    pallas_call x1, Pallas kernels: 50.9 us -> 47.4 us  [on_device(): pl.pallas_call(mix_kernel, name='mix', out_shape=(moved, jax.ShapeDtypeSt...]
    pallas_call x1, Pallas kernels: 19.4 us -> 18.2 us  [on_device(): pl.pallas_call(back_kernel, name='back', out_shape=jax.ShapeDtypeStruct((...]
where the time goes in v4:
time: 72 us; the launch traced here: 71.2 us
  Pallas kernels  70.3 us (98%)
  local copies, waits for them, and re-layouts  0.84 us (1%)
    pallas_call x1, Pallas kernels, on_device(): pl.pallas_call(mix_kernel, name='mix', out_shape=(moved, jax.ShapeDtypeSt...  47.4 us
    pallas_call x1, Pallas kernels, on_device(): pl.pallas_call(back_kernel, name='back', out_shape=jax.ShapeDtypeStruct((...  18.2 us
    pallas_call x1, Pallas kernels, list_call(): pl.pallas_call(list_kernel, name='list', out_shape=(shape((OWNERS, OWNED,...  4.71 us

profile of v4, /device:TPU:1, one launch (start us, length us, event | category | flops | bytes accessed | tf_op | source)
XLA Modules:
  0.0 71.2 jit_solution(5529940942280015556)
XLA Ops:
  0.0 47.4 %mix.1 = (bf16[16,5,32,128]{3,2,1,0:T(8,128)(2,1)S(1)}, bf16[16,5,64,128]{3,2,1,0:T(8,128)(2,1)S(1)}) custom-call(bf16[20,128,128]{2,1,0:T(8,128)(2,1)} %bitcast.3, s32[64]{0:T(128)} %table_in.3, s32[64,128]{1,0:T(8,128)} %bitcast.5, s32[8192]{0:T(1024)} %train_in.1, bf16[128,384]{1,0:T(8,128)(2,1)} %wqkv_in.2, bf16[128,128]{1,0:T(8,128)(2,1)} %wout_in.2), custom_call_target="tpu_custom_call" | custom-call | tf_op jit(solution)/shard_map/mix/pallas_call | solution.py:706
  47.4 4.7 %list.1 = (bf16[16,5,32,128]{3,2,1,0:T(8,128)(2,1)S(1)}, bf16[4,5,256,256]{3,2,1,0:T(8,128)(2,1)S(1)}, f32[4,256,128]{2,1,0:T(8,128)S(1)}, f32[4,5,1,512]{3,2,1,...) custom-call(bf16[16,5,32,128]{3,2,1,0:T(8,128)(2,1)S(1)} %get-tuple-element.13.q_in, ...), custom_call_target="tpu_custom_call" | custom-call | tf_op jit(solution)/shard_map/list/pallas_call | solution.py:672
  52.1 18.2 %back.1 = bf16[32,80,128]{2,1,0:T(8,128)(2,1)S(1)} custom-call(bf16[16,5,32,128]{3,2,1,0:T(8,128)(2,1)S(1)} %get-tuple-element.13.q_in, bf16[16,5,32,128]{3,2,1,0:T(8,128)(2,1)S(1)} %get-tuple-element.15.qp, bf16[4,5,256,256]{3,2,1,0:T(8,128)(2,1)S(1)} %get-tuple-element.16.kv_first, f32[4,256,128]{2,1,0:T(8,128)S(1)} %get-tuple-element.17.bias_first, ...), custom_call_target="tpu_custom_call" | custom-call | tf_op jit(solution)/shard_map/back/pallas_call | solution.py:751
  70.3 0.8 %copy.10 = bf16[32,80,128]{2,1,0:T(8,128)(2,1)} copy(bf16[32,80,128]{2,1,0:T(8,128)(2,1)S(1)} %back.1) | data formatting | bytes 1310720

commit v5 on v4

--- a/solution.py
+++ b/solution.py
@@ -74,8 +74,8 @@
 
 
 def mix_kernel(
-    cells, table_in, live_in, train_in, wqkv_in, wout_in, q_out, kv_out,
-    table, live, train, wqkv, wout, in_sem, own, xbuf, part, level, mean_of, inv_of, st_src, sxy, sz_src, sz, counts, nrm, rows, qkv, att, mix, send,
+    cells, table_in, live_in, train_in, wqkv_in, wout_in, item_in, q_out, qp, kvp,
+    kv_out, key_rows, key_qkv, item_w, table, live, train, wqkv, wout, in_sem, own, xbuf, part, level, mean_of, inv_of, st_src, sxy, sz_src, sz, counts, nrm, rows, qkv, att, mix, send,
     key_wide, key_send, key_in,
     own_sem, xs, xr, ss, sr, zs, zr, ks, kr, qs, qr, rs, rr, ls, lr, ps, pr,
 ):
@@ -87,7 +87,8 @@
     loads = [
         pltpu.make_async_copy(source, target, in_sem.at[i])
         for i, (source, target) in enumerate(
-            ((live_in, live), (table_in, table), (train_in, train), (wqkv_in, wqkv), (wout_in, wout))
+            ((live_in, live), (table_in, table), (train_in, train), (wqkv_in, wqkv), (wout_in, wout),
+             (item_in, item_w))
         )
     ]
     for load in loads:
@@ -200,8 +201,8 @@
         for j in range(KEEP):
             spots[j] = jnp.where((flag == 1) & (seen == j), r, spots[j])
         seen = seen + flag
-    mine = table[row]
-    weights = [jnp.where(table[b] == mine, 1.0, 0.0).astype(F32) for b in range(BLOCKS)]
+    here_table = table[row]
+    weights = [jnp.where(table[b] == here_table, 1.0, 0.0).astype(F32) for b in range(BLOCKS)]
     entries_all = jnp.zeros((1, WIDTH), F32)
     for b in range(BLOCKS):
         entries_all = entries_all + weights[b] * counts[b : b + 1, :]
@@ -246,24 +247,11 @@
 
     lax.fori_loop(0, GROUP, by_row, 0, unroll=8)
 
-    def project(i, none):
-        some = rows[pl.ds(i * 4, 4)].reshape(4 * FEATS, WIDTH)
-        out = jnp.dot(some, wqkv[...], preferred_element_type=F32)
-        qkv[pl.ds(i * 4, 4), :, 0:WIDTH] = (
-            (out[:, :WIDTH] * SCALE).astype(BF16).reshape(4, FEATS, WIDTH)
-        )
-        qkv[pl.ds(i * 4, 4), :, WIDTH:] = (
-            out[:, WIDTH:].astype(BF16).reshape(4, FEATS, 2 * WIDTH)
-        )
-        return none
-
-    lax.fori_loop(0, GROUP // 4, project, 0, unroll=4)
-
     head = iota((FEATS, WIDTH), 1) // HEAD_DIM
-    def attended(r):
-        query = qkv[r, :, 0:WIDTH]
-        key = qkv[r, :, WIDTH : 2 * WIDTH]
-        value = qkv[r, :, 2 * WIDTH :]
+    def attended(source, r):
+        query = source[r, :, 0:WIDTH]
+        key = source[r, :, WIDTH : 2 * WIDTH]
+        value = source[r, :, 2 * WIDTH :]
         keys = jnp.concatenate(
             [jnp.where(head == h, key, jnp.zeros_like(key)) for h in range(HEADS)], axis=0
         )
@@ -285,11 +273,19 @@
             preferred_element_type=F32,
         ).astype(BF16)
 
-    found = [attended(spot) for spot in spots]
     for j in range(KEEP):
-        out = jnp.dot(found[j], wout[...], preferred_element_type=F32)
-        out = out + rows[spots[j]].astype(F32)
-        key_wide[pl.ds(KEEP * lax.rem(x, 2) + j, FEATS, stride=8), :] = out
+        key_rows[j] = rows[spots[j]]
+    some = key_rows[...].reshape(KEEP * FEATS, WIDTH)
+    out = jnp.dot(some, wqkv[...], preferred_element_type=F32)
+    key_qkv[:, :, 0:WIDTH] = (out[:, :WIDTH] * SCALE).astype(BF16).reshape(KEEP, FEATS, WIDTH)
+    key_qkv[:, :, WIDTH:] = out[:, WIDTH:].astype(BF16).reshape(KEEP, FEATS, 2 * WIDTH)
+    found = jnp.concatenate([attended(key_qkv, j) for j in range(KEEP)], axis=0)
+    out = jnp.dot(found, wout[...], preferred_element_type=F32)
+    out = out + key_rows[...].reshape(KEEP * FEATS, WIDTH).astype(F32)
+    for j in range(KEEP):
+        key_wide[pl.ds(KEEP * lax.rem(x, 2) + j, FEATS, stride=8), :] = out[
+            j * FEATS : (j + 1) * FEATS
+        ]
     key_send[...] = key_wide[...].reshape(FEATS, 8, WIDTH).astype(BF16)
     peers = []
     for dy in range(YS):
@@ -307,17 +303,29 @@
         key_moved.append(copy)
     key_in[owner] = key_send[pl.ds(owner * OWNED, OWNED)]
 
+    def project(i, none):
+        some = rows[pl.ds(i * 4, 4)].reshape(4 * FEATS, WIDTH)
+        out = jnp.dot(some, wqkv[...], preferred_element_type=F32)
+        qkv[pl.ds(i * 4, 4), :, 0:WIDTH] = (
+            (out[:, :WIDTH] * SCALE).astype(BF16).reshape(4, FEATS, WIDTH)
+        )
+        qkv[pl.ds(i * 4, 4), :, WIDTH:] = (
+            out[:, WIDTH:].astype(BF16).reshape(4, FEATS, 2 * WIDTH)
+        )
+        return none
+
+    lax.fori_loop(0, GROUP // 4, project, 0, unroll=4)
+
     moved = []
 
-    def half(part):
-        first_row = part * (GROUP // 2)
-
+    def attend_rows(low, size):
         def attend(r, none):
-            att[r] = attended(r)
+            att[r] = attended(qkv, r)
             return none
 
-        lax.fori_loop(first_row, first_row + GROUP // 2, attend, 0, unroll=16)
-
+        lax.fori_loop(low, low + size, attend, 0, unroll=size)
+
+    def send_rows(low, size):
         def update(i, none):
             some = att[pl.ds(i * 4, 4)].reshape(4 * FEATS, WIDTH)
             out = jnp.dot(some, wout[...], preferred_element_type=F32)
@@ -325,32 +333,33 @@
             mix[pl.ds(i * 4 * FEATS, 4 * FEATS), :] = out
             return none
 
-        lax.fori_loop(part * 4, part * 4 + 4, update, 0, unroll=2)
+        lax.fori_loop(low // 4, (low + size) // 4, update, 0, unroll=2)
 
         def turn(f, none):
-            send[f, first_row : first_row + GROUP // 2, :] = mix[
-                pl.ds(first_row * FEATS + f, GROUP // 2, stride=FEATS), :
+            send[f, low : low + size, :] = mix[
+                pl.ds(low * FEATS + f, size, stride=FEATS), :
             ].astype(BF16)
             return none
 
         lax.fori_loop(0, FEATS, turn, 0, unroll=8)
-        these = pl.ds(first_row, GROUP // 2)
+        these = pl.ds(low, size)
         for k, to, to_row, tx in peers:
+            at = (low // 8) * OWNERS + k
             copy = remote(
                 send.at[pl.ds(to * OWNED, OWNED), these],
                 q_out.at[owner, :, these],
-                qs.at[part * OWNERS + k],
-                qr.at[part * OWNERS + k],
+                qs.at[at],
+                qr.at[at],
                 to_row,
                 tx,
             )
             copy.start()
             moved.append(copy)
-        q_out[owner, :, first_row : first_row + GROUP // 2, :] = send[
-            pl.ds(owner * OWNED, OWNED), first_row : first_row + GROUP // 2, :
+        q_out[owner, :, low : low + size, :] = send[
+            pl.ds(owner * OWNED, OWNED), low : low + size, :
         ]
 
-    half(0)
+    attend_rows(0, 16)
 
     for copy in key_moved:
         copy.wait_recv()
@@ -397,9 +406,7 @@
     for i in range(count):
         over(0, i)
 
-    half(1)
-
-    for k in range(4):
+    def ring_step(k):
         for i in range(count):
             if on_right(k, i):
                 lands(-1 - k, i, (rs, rr), k, right)
@@ -411,15 +418,56 @@
                 if on_left(k + 1, i):
                     hop(1 + k, i, (ls, lr), k + 1, left)
                 over(1 + k if k < 3 else -4, i)
+
+    def project_place(at):
+        some = kv_out[at].reshape(OWNED * KEYS, WIDTH)
+        got = jnp.dot(some, item_w[:, WIDTH:], preferred_element_type=F32)
+        kvp[at] = got.astype(BF16).reshape(OWNED, KEYS, 2 * WIDTH)
+
+    def mine(d):
+        project_place(around(z, d, ZS) * CS + c)
+
+    def others(d):
+        at = around(z, d, ZS) * CS + 1 - c
+        for i in range(count):
+            came = kv_out.at[at, pl.ds(CHUNKS[i][0], CHUNKS[i][1])]
+            k = (d + 4) * count + i
+            remote(came, came, ps.at[k], pr.at[k], other, x).wait_recv()
+        project_place(at)
+
+    send_rows(0, 16)
+    attend_rows(16, 8)
+    send_rows(16, 8)
+    ring_step(0)
+    attend_rows(24, 8)
+    send_rows(24, 8)
+    ring_step(1)
+    for d in (0, -1, 1):
+        mine(d)
+    others(0)
+    ring_step(2)
     for copy in moved:
         copy.wait_recv()
-    for d in range(-4, 4):
-        for i in range(count):
-            came = kv_out.at[
-                around(z, d, ZS) * CS + 1 - c, pl.ds(CHUNKS[i][0], CHUNKS[i][1])
-            ]
-            at = (d + 4) * count + i
-            remote(came, came, ps.at[at], pr.at[at], other, x).wait_recv()
+
+    def project_q(i, none):
+        some = q_out[i].reshape(OWNED * GROUP, WIDTH)
+        got = jnp.dot(some, item_w[:, :WIDTH], preferred_element_type=F32)
+        qp[i] = (got * SCALE).astype(BF16).reshape(OWNED, GROUP, WIDTH)
+        return none
+
+    lax.fori_loop(0, OWNERS, project_q, 0, unroll=4)
+    mine(-2)
+    mine(2)
+    others(-1)
+    others(1)
+    ring_step(3)
+    others(-2)
+    others(2)
+    mine(-3)
+    mine(3)
+    mine(-4)
+    for d in (-3, 3, -4):
+        others(d)
 
     for copy in stat_xy + [copy for _, copy in bulk] + stat_z + key_moved + moved + sent:
         copy.wait_send()
@@ -453,15 +501,15 @@
 
 
 def list_kernel(
-    q_in, kv_in, table_in, train_in, wqkv_in,
-    qp, kv_first, bias_first, tops, totals, accs,
-    table, train, wqkv, in_sem, kvp, kv_more, bias_more, every, chosen,
+    qp, kvp, table_in, train_in,
+    kv_first, bias_first, tops, totals, accs,
+    table, train, in_sem, kv_more, bias_more, every, chosen,
 ):
     row, x, y, z, c = position()
     loads = [
         pltpu.make_async_copy(source, target, in_sem.at[i])
         for i, (source, target) in enumerate(
-            ((wqkv_in, wqkv), (table_in, table), (train_in, train))
+            ((table_in, table), (train_in, train))
         )
     ]
     for load in loads:
@@ -471,22 +519,6 @@
     accs[...] = jnp.zeros_like(accs)
     for load in loads:
         load.wait()
-
-    def project_q(i, none):
-        part = q_in[i].reshape(OWNED * GROUP, WIDTH)
-        got = jnp.dot(part, wqkv[:, :WIDTH], preferred_element_type=F32)
-        qp[i] = (got * SCALE).astype(BF16).reshape(OWNED, GROUP, WIDTH)
-        return none
-
-    lax.fori_loop(0, OWNERS, project_q, 0, unroll=4)
-
-    def project_kv(i, none):
-        part = kv_in[i].reshape(OWNED * KEYS, WIDTH)
-        got = jnp.dot(part, wqkv[:, WIDTH:], preferred_element_type=F32)
-        kvp[i] = got.astype(BF16).reshape(OWNED, KEYS, 2 * WIDTH)
-        return none
-
-    lax.fori_loop(0, PLACES, project_kv, 0, unroll=4)
 
     group = (iota((OWNERS, BLOCK), 1) // GROUP == iota((OWNERS, BLOCK), 0) // KEEP)
     spread = train[...].astype(F32)[:, None, :] * group.astype(F32)[None]
@@ -666,35 +698,32 @@
         copy.wait_send()
 
 
-def list_call(query, key, block_table, train, item_qkv):
+def list_call(query, key, block_table, train):
     shape = jax.ShapeDtypeStruct
     state = shape((YS, OWNED, 1, HEADS * BLOCK), F32)
     return pl.pallas_call(
         list_kernel,
         name="list",
         out_shape=(
-            shape((OWNERS, OWNED, GROUP, WIDTH), BF16),
             shape((YS, OWNED, TILE, 2 * WIDTH), BF16),
             shape((YS, TILE, WIDTH), F32),
             state,
             state,
             shape((YS, OWNED, WIDTH, BLOCK), F32),
         ),
-        in_specs=[VMEM, VMEM, HBM, HBM, HBM],
-        out_specs=(VMEM,) * 6,
+        in_specs=[VMEM, VMEM, HBM, HBM],
+        out_specs=(VMEM,) * 5,
         scratch_shapes=[
             pltpu.SMEM((BLOCKS,), jnp.int32),
             pltpu.VMEM((BLOCKS, BLOCK), jnp.int32),
-            pltpu.VMEM((WIDTH, 3 * WIDTH), BF16),
-            pltpu.SemaphoreType.DMA((3,)),
-            pltpu.VMEM((PLACES, OWNED, KEYS, 2 * WIDTH), BF16),
+            pltpu.SemaphoreType.DMA((2,)),
             pltpu.VMEM((OWNED, PLACES * KEYS, 2 * WIDTH), BF16),
             pltpu.VMEM((PLACES * KEYS, WIDTH), F32),
             pltpu.VMEM((PLACES * KEYS, WIDTH), F32),
             pltpu.SMEM((BLOCKS + 8,), jnp.int32),
         ],
         compiler_params=pltpu.CompilerParams(vmem_limit_bytes=ITEM_VMEM),
-    )(query, key, *stay(block_table, train, item_qkv))
+    )(query, key, *stay(block_table, train))
 
 
 def on_device(cells, block_table, row_live, row_train, feat_qkv, feat_out, item_qkv, item_out):
@@ -703,19 +732,27 @@
     by_feature = jnp.transpose(cells, (1, 0, 2))
     dma = pltpu.SemaphoreType.DMA
     moved = jax.ShapeDtypeStruct((OWNERS, OWNED, GROUP, WIDTH), BF16)
-    query, key = pl.pallas_call(
+    mixed, query, key = pl.pallas_call(
         mix_kernel,
         name="mix",
-        out_shape=(moved, jax.ShapeDtypeStruct((PLACES, OWNED, KEYS, WIDTH), BF16)),
-        in_specs=[HBM] * 6,
-        out_specs=(VMEM, VMEM),
+        out_shape=(
+            moved,
+            moved,
+            jax.ShapeDtypeStruct((PLACES, OWNED, KEYS, 2 * WIDTH), BF16),
+        ),
+        in_specs=[HBM] * 7,
+        out_specs=(VMEM,) * 3,
         scratch_shapes=[
+            pltpu.VMEM((PLACES, OWNED, KEYS, WIDTH), BF16),
+            pltpu.VMEM((KEEP, FEATS, WIDTH), BF16),
+            pltpu.VMEM((KEEP, FEATS, 3 * WIDTH), BF16),
+            pltpu.VMEM((WIDTH, 3 * WIDTH), BF16),
             pltpu.SMEM((BLOCKS,), jnp.int32),
             pltpu.VMEM((BLOCKS, BLOCK), jnp.int32),
             pltpu.SMEM((BLOCKS * BLOCK,), jnp.int32),
             pltpu.VMEM((WIDTH, 3 * WIDTH), BF16),
             pltpu.VMEM((WIDTH, WIDTH), BF16),
-            dma((5,)),
+            dma((6,)),
             pltpu.VMEM((SHARD, BLOCK, WIDTH), BF16),
             pltpu.VMEM((FEATS, GROUP, WIDTH), BF16),
             pltpu.VMEM((SHARD, WIDTH), F32),
@@ -739,15 +776,15 @@
             dma((2,)),
             dma((XS,)), dma((XS,)), dma((OWNERS * CS,)), dma((OWNERS * CS,)),
             dma((8,)), dma((8,)),
-            dma((OWNERS,)), dma((OWNERS,)), dma((2 * OWNERS,)), dma((2 * OWNERS,)),
+            dma((OWNERS,)), dma((OWNERS,)), dma((4 * OWNERS,)), dma((4 * OWNERS,)),
             dma((4 * OWNED,)), dma((4 * OWNED,)), dma((4 * OWNED,)), dma((4 * OWNED,)),
             dma((8 * OWNED,)), dma((8 * OWNED,)),
         ],
         compiler_params=pltpu.CompilerParams(
             collective_id=0, has_side_effects=True, vmem_limit_bytes=MIX_VMEM
         ),
-    )(*stay(by_feature, block_table, live, row_train, feat_qkv, feat_out))
-    listed = list_call(query, key, block_table, train, item_qkv)
+    )(*stay(by_feature, block_table, live, row_train, feat_qkv, feat_out, item_qkv))
+    listed = list_call(query, key, block_table, train)
     return pl.pallas_call(
         back_kernel,
         name="back",
@@ -764,7 +801,7 @@
         compiler_params=pltpu.CompilerParams(
             collective_id=1, has_side_effects=True, vmem_limit_bytes=BACK_VMEM
         ),
-    )(query, *listed, *stay(item_out))
+    )(mixed, query, *listed, *stay(item_out))
 
 
 def solution(mesh):

time: 72 us -> 68.9 us (0.957)
  Pallas kernels: 70.3 us -> 67.8 us
    pallas_call x2, Pallas kernels: 52.1 us -> 49.7 us  [the longest x1 47.2 us: on_device(): pl.pallas_call(mix_kernel, name='mix', out_shape=(moved, moved, jax.Shape...]
where the time goes in v5:
time: 68.9 us; the launch traced here: 68.6 us
  Pallas kernels  67.8 us (98%)
  local copies, waits for them, and re-layouts  0.84 us (1%)
    pallas_call x1, Pallas kernels, on_device(): pl.pallas_call(mix_kernel, name='mix', out_shape=(moved, moved, jax.Shape...  47.2 us
    pallas_call x1, Pallas kernels, on_device(): pl.pallas_call(back_kernel, name='back', out_shape=jax.ShapeDtypeStruct((...  18 us
    pallas_call x1, Pallas kernels, list_call(): pl.pallas_call(list_kernel, name='list', out_shape=(shape((YS, OWNED, TIL...  2.5 us

profile of v5, /device:TPU:1, one launch (start us, length us, event | category | flops | bytes accessed | tf_op | source)
XLA Modules:
  0.0 68.6 jit_solution(9352962605228316728)
XLA Ops:
  0.0 47.2 %mix.1 = (bf16[16,5,32,128]{3,2,1,0:T(8,128)(2,1)S(1)}, bf16[16,5,32,128]{3,2,1,0:T(8,128)(2,1)S(1)}, bf16[16,5,64,256]{3,2,1,0:T(8,128)(2,1)S(1)}) custom-call(bf16[20,128,128]{2,1,0:T(8,128)(2,1)} %bitcast.3, s32[64]{0:T(128)} %table_in.3, s32[64,128]{1,0:T(8,128)} %bitcast.5, s32[8192]{0:T(1024)} %train_in.1, bf16[128,384]{1,0:T(8,128)(2,1)} %wqkv_in.1, ...), custom_call_target="tpu_custom_call" | custom-call | tf_op jit(solution)/shard_map/mix/pallas_call | solution.py:735
  47.2 2.5 %list.1 = (bf16[4,5,256,256]{3,2,1,0:T(8,128)(2,1)S(1)}, f32[4,256,128]{2,1,0:T(8,128)S(1)}, f32[4,5,1,512]{3,2,1,0:T(1,128)S(1)}, f32[4,5,1,512]{3,2,1,0:T(1,128)S(1)}, f32[4,5,128,128]{3,2,1,0:T(8,128)S(1)}) custom-call(bf16[16,5,32,128]{3,2,1,0:T(8,128)(2,1)S(1)} %get-tuple-element.14.qp, bf16[16,5,64,256]{3,2,1,0:T(8,128)(2,1)S(1)} %get-tuple-element.15.kvp, ...), custom_call_target="tpu_custom_call" | custom-call | tf_op jit(solution)/shard_map/list/pallas_call | solution.py:704
  49.8 18.0 %back.1 = bf16[32,80,128]{2,1,0:T(8,128)(2,1)S(1)} custom-call(bf16[16,5,32,128]{3,2,1,0:T(8,128)(2,1)S(1)} %get-tuple-element.13.q_in, bf16[16,5,32,128]{3,2,1,0:T(8,128)(2,1)S(1)} %get-tuple-element.14.qp, bf16[4,5,256,256]{3,2,1,0:T(8,128)(2,1)S(1)} %get-tuple-element.16.kv_first, f32[4,256,128]{2,1,0:T(8,128)S(1)} %get-tuple-element.17.bias_first, ...), custom_call_target="tpu_custom_call" | custom-call | tf_op jit(solution)/shard_map/back/pallas_call | solution.py:788
  67.8 0.8 %copy.10 = bf16[32,80,128]{2,1,0:T(8,128)(2,1)} copy(bf16[32,80,128]{2,1,0:T(8,128)(2,1)S(1)} %back.1) | data formatting | bytes 1310720

commit v6 on v5

--- a/solution.py
+++ b/solution.py
@@ -24,8 +24,6 @@
 MASKED = -1e30
 SCALE = HEAD_DIM**-0.5 * 1.4426950408889634
 MESH = pl.DeviceIdType.MESH
-CHUNKS = ((0, 1), (1, 1), (2, 1), (3, 1), (4, 1))
-FROM_RIGHT = 3
 MIX_VMEM = 20 << 20
 ITEM_VMEM = 20 << 20
 BACK_VMEM = 12 << 20
@@ -375,49 +373,58 @@
     right, left = row_of(y, around(z, 1, ZS), c), row_of(y, around(z, -1, ZS), c)
     other = row_of(y, z, 1 - c)
 
-    count = len(CHUNKS)
-
-    def slot(d, i):
-        return kv_out.at[around(z, d, ZS) * CS + c, pl.ds(CHUNKS[i][0], CHUNKS[i][1])]
-
-    def hop(d, i, sems, k, to):
-        send_sems, recv_sems = sems
-        at = k * count + i
-        copy = remote(slot(d, i), slot(d, i), send_sems.at[at], recv_sems.at[at], to, x)
+    right_two, left_two = row_of(y, around(z, 2, ZS), c), row_of(y, around(z, -2, ZS), c)
+
+    def part_of(d, features):
+        return kv_out.at[around(z, d, ZS) * CS + c, pl.ds(*features)]
+
+    def hop(d, features, sems, k, to):
+        here_part = part_of(d, features)
+        copy = remote(here_part, here_part, sems[0].at[k], sems[1].at[k], to, x)
         copy.start()
         sent.append(copy)
 
-    def lands(d, i, sems, k, to):
-        at = k * count + i
-        remote(slot(d, i), slot(d, i), sems[0].at[at], sems[1].at[at], to, x).wait_recv()
-
-    def over(d, i):
-        hop(d, i, (ps, pr), d + 4, other)
-
-    def on_right(k, i):
-        return k < 3 or (k == 3 and i < FROM_RIGHT)
-
-    def on_left(k, i):
-        return k < 3 or (k == 3 and i >= FROM_RIGHT)
-
-    for i in range(count):
-        hop(0, i, (rs, rr), 0, right)
-        hop(0, i, (ls, lr), 0, left)
-    for i in range(count):
-        over(0, i)
+    def lands(d, features, sems, k):
+        here_part = part_of(d, features)
+        remote(here_part, here_part, sems[0].at[k], sems[1].at[k], right, x).wait_recv()
+
+    every_feature, low_features, high_features = (0, OWNED), (0, 3), (3, OWNED - 3)
+
+    def place_at(d, core):
+        return kv_out.at[around(z, d, ZS) * CS + core]
+
+    def over(d):
+        whole = place_at(d, c)
+        copy = remote(whole, whole, ps.at[d + 4], pr.at[d + 4], other, x)
+        copy.start()
+        sent.append(copy)
+
+    hop(0, every_feature, (rs, rr), 0, right)
+    hop(0, every_feature, (ls, lr), 0, left)
+    hop(0, every_feature, (rs, rr), 1, right_two)
+    hop(0, every_feature, (ls, lr), 1, left_two)
+    over(0)
 
     def ring_step(k):
-        for i in range(count):
-            if on_right(k, i):
-                lands(-1 - k, i, (rs, rr), k, right)
-                if on_right(k + 1, i):
-                    hop(-1 - k, i, (rs, rr), k + 1, right)
-                over(-1 - k, i)
-            if on_left(k, i):
-                lands(1 + k, i, (ls, lr), k, left)
-                if on_left(k + 1, i):
-                    hop(1 + k, i, (ls, lr), k + 1, left)
-                over(1 + k if k < 3 else -4, i)
+        if k == 0:
+            lands(-1, every_feature, (rs, rr), 0)
+            hop(-1, every_feature, (rs, rr), 2, right_two)
+            lands(1, every_feature, (ls, lr), 0)
+            hop(1, every_feature, (ls, lr), 2, left_two)
+        if k == 1:
+            lands(-2, every_feature, (rs, rr), 1)
+            hop(-2, low_features, (rs, rr), 3, right_two)
+            lands(2, every_feature, (ls, lr), 1)
+            hop(2, high_features, (ls, lr), 3, left_two)
+        if k == 2:
+            lands(-3, every_feature, (rs, rr), 2)
+            lands(3, every_feature, (ls, lr), 2)
+        if k == 3:
+            lands(-4, low_features, (rs, rr), 3)
+            lands(-4, high_features, (ls, lr), 3)
+        over(-1 - k)
+        if k < 3:
+            over(1 + k)
 
     def project_place(at):
         some = kv_out[at].reshape(OWNED * KEYS, WIDTH)
@@ -428,12 +435,9 @@
         project_place(around(z, d, ZS) * CS + c)
 
     def others(d):
-        at = around(z, d, ZS) * CS + 1 - c
-        for i in range(count):
-            came = kv_out.at[at, pl.ds(CHUNKS[i][0], CHUNKS[i][1])]
-            k = (d + 4) * count + i
-            remote(came, came, ps.at[k], pr.at[k], other, x).wait_recv()
-        project_place(at)
+        came = place_at(d, 1 - c)
+        remote(came, came, ps.at[d + 4], pr.at[d + 4], other, x).wait_recv()
+        project_place(around(z, d, ZS) * CS + 1 - c)
 
     send_rows(0, 16)
     attend_rows(16, 8)
@@ -777,8 +781,8 @@
             dma((XS,)), dma((XS,)), dma((OWNERS * CS,)), dma((OWNERS * CS,)),
             dma((8,)), dma((8,)),
             dma((OWNERS,)), dma((OWNERS,)), dma((4 * OWNERS,)), dma((4 * OWNERS,)),
-            dma((4 * OWNED,)), dma((4 * OWNED,)), dma((4 * OWNED,)), dma((4 * OWNED,)),
-            dma((8 * OWNED,)), dma((8 * OWNED,)),
+            dma((4,)), dma((4,)), dma((4,)), dma((4,)),
+            dma((8,)), dma((8,)),
         ],
         compiler_params=pltpu.CompilerParams(
             collective_id=0, has_side_effects=True, vmem_limit_bytes=MIX_VMEM

time: 68.9 us -> 67.9 us (0.985)
  the two profiles are of different devices: /device:TPU:1 before, /device:TPU:32 now
where the time goes in v6:
time: 67.9 us; the launch traced here: 67.6 us
  Pallas kernels  66.8 us (98%)
  local copies, waits for them, and re-layouts  0.84 us (1%)
    pallas_call x1, Pallas kernels, on_device(): pl.pallas_call(mix_kernel, name='mix', out_shape=(moved, moved, jax.Shape...  43.2 us
    pallas_call x1, Pallas kernels, on_device(): pl.pallas_call(back_kernel, name='back', out_shape=jax.ShapeDtypeStruct((...  21.2 us
    pallas_call x1, Pallas kernels, list_call(): pl.pallas_call(list_kernel, name='list', out_shape=(shape((YS, OWNED, TIL...  2.38 us

profile of v6, /device:TPU:32, one launch (start us, length us, event | category | flops | bytes accessed | tf_op | source)
XLA Modules:
  0.0 67.6 jit_solution(7214590481876583818)
XLA Ops:
  0.0 43.2 %mix.1 = (bf16[16,5,32,128]{3,2,1,0:T(8,128)(2,1)S(1)}, bf16[16,5,32,128]{3,2,1,0:T(8,128)(2,1)S(1)}, bf16[16,5,64,256]{3,2,1,0:T(8,128)(2,1)S(1)}) custom-call(bf16[20,128,128]{2,1,0:T(8,128)(2,1)} %bitcast.3, s32[64]{0:T(128)} %table_in.3, s32[64,128]{1,0:T(8,128)} %bitcast.5, s32[8192]{0:T(1024)} %train_in.1, bf16[128,384]{1,0:T(8,128)(2,1)} %wqkv_in.1, ...), custom_call_target="tpu_custom_call" | custom-call | tf_op jit(solution)/shard_map/mix/pallas_call | solution.py:739
  43.2 2.4 %list.1 = (bf16[4,5,256,256]{3,2,1,0:T(8,128)(2,1)S(1)}, f32[4,256,128]{2,1,0:T(8,128)S(1)}, f32[4,5,1,512]{3,2,1,0:T(1,128)S(1)}, f32[4,5,1,512]{3,2,1,0:T(1,128)S(1)}, f32[4,5,128,128]{3,2,1,0:T(8,128)S(1)}) custom-call(bf16[16,5,32,128]{3,2,1,0:T(8,128)(2,1)S(1)} %get-tuple-element.14.qp, bf16[16,5,64,256]{3,2,1,0:T(8,128)(2,1)S(1)} %get-tuple-element.15.kvp, ...), custom_call_target="tpu_custom_call" | custom-call | tf_op jit(solution)/shard_map/list/pallas_call | solution.py:708
  45.6 21.2 %back.1 = bf16[32,80,128]{2,1,0:T(8,128)(2,1)S(1)} custom-call(bf16[16,5,32,128]{3,2,1,0:T(8,128)(2,1)S(1)} %get-tuple-element.13.q_in, bf16[16,5,32,128]{3,2,1,0:T(8,128)(2,1)S(1)} %get-tuple-element.14.qp, bf16[4,5,256,256]{3,2,1,0:T(8,128)(2,1)S(1)} %get-tuple-element.16.kv_first, f32[4,256,128]{2,1,0:T(8,128)S(1)} %get-tuple-element.17.bias_first, ...), custom_call_target="tpu_custom_call" | custom-call | tf_op jit(solution)/shard_map/back/pallas_call | solution.py:792
  66.8 0.8 %copy.10 = bf16[32,80,128]{2,1,0:T(8,128)(2,1)} copy(bf16[32,80,128]{2,1,0:T(8,128)(2,1)S(1)} %back.1) | data formatting | bytes 1310720

commit v7 on v6

--- a/solution.py
+++ b/solution.py
@@ -155,7 +155,7 @@
         copy.start()
         stat_xy.append(copy)
     bulk = []
-    for d in (1, 3, 2):
+    for d in (2, 1, 3):
         to = around(x, d, XS)
         copy = remote(
             cells.at[:, pl.ds(pl.multiple_of(to * GROUP, GROUP), GROUP)],
@@ -291,6 +291,7 @@
             if dx or dy:
                 ty, tx = around(y, dy, YS), around(x, dx, XS)
                 peers.append((dy * XS + dx, ty * XS + tx, row_of(ty, z, c), tx))
+    peers.sort(key=lambda peer: -min(peer[0] // XS, YS - peer[0] // XS) - min(peer[0] % XS, XS - peer[0] % XS))
     sent = []
     key_moved = []
     for k, to, to_row, tx in peers:

time: 67.9 us -> 69.2 us (1.019)
  the two profiles are of different devices: /device:TPU:32 before, /device:TPU:1 now
where the time goes in v7:
time: 69.2 us; the launch traced here: 68.7 us
  Pallas kernels  67.8 us (98%)
  local copies, waits for them, and re-layouts  0.84 us (1%)
    pallas_call x1, Pallas kernels, on_device(): pl.pallas_call(mix_kernel, name='mix', out_shape=(moved, moved, jax.Shape...  47.4 us
    pallas_call x1, Pallas kernels, on_device(): pl.pallas_call(back_kernel, name='back', out_shape=jax.ShapeDtypeStruct((...  17.9 us
    pallas_call x1, Pallas kernels, list_call(): pl.pallas_call(list_kernel, name='list', out_shape=(shape((YS, OWNED, TIL...  2.49 us

profile of v7, /device:TPU:1, one launch (start us, length us, event | category | flops | bytes accessed | tf_op | source)
XLA Modules:
  0.0 68.7 jit_solution(2089384989576353338)
XLA Ops:
  0.0 47.4 %mix.1 = (bf16[16,5,32,128]{3,2,1,0:T(8,128)(2,1)S(1)}, bf16[16,5,32,128]{3,2,1,0:T(8,128)(2,1)S(1)}, bf16[16,5,64,256]{3,2,1,0:T(8,128)(2,1)S(1)}) custom-call(bf16[20,128,128]{2,1,0:T(8,128)(2,1)} %bitcast.3, s32[64]{0:T(128)} %table_in.3, s32[64,128]{1,0:T(8,128)} %bitcast.5, s32[8192]{0:T(1024)} %train_in.1, bf16[128,384]{1,0:T(8,128)(2,1)} %wqkv_in.1, ...), custom_call_target="tpu_custom_call" | custom-call | tf_op jit(solution)/shard_map/mix/pallas_call | solution.py:740
  47.4 2.5 %list.1 = (bf16[4,5,256,256]{3,2,1,0:T(8,128)(2,1)S(1)}, f32[4,256,128]{2,1,0:T(8,128)S(1)}, f32[4,5,1,512]{3,2,1,0:T(1,128)S(1)}, f32[4,5,1,512]{3,2,1,0:T(1,128)S(1)}, f32[4,5,128,128]{3,2,1,0:T(8,128)S(1)}) custom-call(bf16[16,5,32,128]{3,2,1,0:T(8,128)(2,1)S(1)} %get-tuple-element.14.qp, bf16[16,5,64,256]{3,2,1,0:T(8,128)(2,1)S(1)} %get-tuple-element.15.kvp, ...), custom_call_target="tpu_custom_call" | custom-call | tf_op jit(solution)/shard_map/list/pallas_call | solution.py:709
  49.9 17.9 %back.1 = bf16[32,80,128]{2,1,0:T(8,128)(2,1)S(1)} custom-call(bf16[16,5,32,128]{3,2,1,0:T(8,128)(2,1)S(1)} %get-tuple-element.13.q_in, bf16[16,5,32,128]{3,2,1,0:T(8,128)(2,1)S(1)} %get-tuple-element.14.qp, bf16[4,5,256,256]{3,2,1,0:T(8,128)(2,1)S(1)} %get-tuple-element.16.kv_first, f32[4,256,128]{2,1,0:T(8,128)S(1)} %get-tuple-element.17.bias_first, ...), custom_call_target="tpu_custom_call" | custom-call | tf_op jit(solution)/shard_map/back/pallas_call | solution.py:793
  67.8 0.8 %copy.10 = bf16[32,80,128]{2,1,0:T(8,128)(2,1)} copy(bf16[32,80,128]{2,1,0:T(8,128)(2,1)S(1)} %back.1) | data formatting | bytes 1310720
